TPU v7x, 256 devices: a whole 4x4x8 slice. The times are simulated.
256 devices in a mesh: row: 8 (over y_lo, x), col: 32 (over z, y_hi, core).
Axes of the slice: x: 4, y: 4 (y_hi: 2, y_lo: 2; y = y_hi * 2 + y_lo), z: 8, core: 2. Of those that a mesh axis runs over, the one named last changes fastest.
Arguments:
- pair_rep: float32 [256, 256, 128], P('row', 'col'), may hold values from -160 to 160
- ln_gain: float32 [128], replicated, may hold values from 0.25 to 1.75
- ln_bias: float32 [128], replicated, may hold values from -3 to 3
- w_in: float32 [1024, 128], replicated, may hold values from -0.5 to 0.5
- w_out: float32 [512, 128], replicated, may hold values from -0.25 to 0.25
- w_pde: float32 [128, 64], replicated, may hold values from -2 to 2
- labels: int32 [256, 256], P('row', 'col'), may hold values from 0 to 63
- pair_mask: int32 [256, 256], P('row', 'col'), may hold values from 0 to 1, as said below
Outputs:
- mean_loss: float32 [], replicated
- d_pair_rep: float32 [256, 256, 128], P('row', 'col')
- d_ln_gain: float32 [128], replicated
- d_ln_bias: float32 [128], replicated
- d_w_in: float32 [1024, 128], P(('row', 'col'))
- d_w_out: float32 [512, 128], P(('row', 'col'))
- d_w_pde: float32 [128, 64], replicated
Inputs may be any that keep to these rules, and one draw needn't show every extreme that they name: pair_mask[i][j] = m_i m_j for a flag m_i of token i, with m_i = 1 whenever i is a multiple of 16.
All inputs are finite; a program needn't handle non-finite values.
Results may differ from a plain program's by a relative error of at most 0.0003.
Values sent between devices are 32-bit elements; how exact they have to be, the bound alone decides.
No kernel may reach another device: no remote copies, remote signals or barrier semaphores. Data moves between devices by JAX's collectives and lax.ppermute only.
A program may use at most 64 MiB of HBM per device.

v0:
```python
import jax
import jax.numpy as jnp
from jax import lax
from jax.sharding import Mesh
from jax.sharding import PartitionSpec as P

ROW = ("row_0", "row_1")
COL = ("col_0", "col_1", "col_2")
ROW_COL = ("row_0", "row_1", "col_0", "col_1", "col_2")


epsilon = 1e-05


def over_axes(shard, axes):
    for axis in axes:
        shard = lax.psum(shard, axis)
    return shard


def in_blocks(shard, dim, size):
    before, after = (shard.shape[:dim], shard.shape[dim + 1 :])
    return jnp.moveaxis(shard.reshape(*before, size, -1, *after), dim, 0)


def sent_and_summed(shard, axis, dim):
    tiles = in_blocks(shard, dim, lax.axis_size(axis))
    arrived = lax.all_to_all(tiles, axis, split_axis=0, concat_axis=0, tiled=True)
    return arrived.sum(axis=0)


def transition(rows_block, ln_gain, ln_bias, w_in, w_out):
    average = jnp.mean(rows_block, axis=-1, keepdims=True)
    centred = rows_block - average
    variance = jnp.mean(centred * centred, axis=-1, keepdims=True)
    normed = centred * lax.rsqrt(variance + epsilon) * ln_gain + ln_bias
    projected_in = lax.dot_general(
        normed,
        w_in,
        (((1,), (1,)), ((), ())),
        precision=lax.Precision.HIGHEST,
        preferred_element_type=jnp.float32,
    )
    hidden_units = w_out.shape[0]
    hidden = jax.nn.silu(projected_in[:, :hidden_units]) * projected_in[:, hidden_units:]
    return rows_block + jnp.dot(
        hidden, w_out, precision=lax.Precision.HIGHEST, preferred_element_type=jnp.float32
    )


def group_rows(tile_rows, tile_cols):
    stride_rows = 1
    while (
        stride_rows < tile_rows
        and stride_rows * tile_cols < 1024
        and (tile_rows % (stride_rows * 2) == 0)
    ):
        stride_rows = stride_rows * 2
    return stride_rows


def mirror(tile):
    row_devices = lax.axis_size(ROW)
    col_devices = lax.axis_size(COL)
    factor = col_devices // row_devices
    tile_cols = tile.shape[1]
    channels = tile.shape[2]
    slab_rows = tile_cols // row_devices
    pieces = tile.reshape(factor, row_devices, slab_rows, tile_cols * channels)
    pieces = lax.all_to_all(
        lax.all_to_all(pieces, ROW, split_axis=1, concat_axis=0, tiled=True),
        COL,
        split_axis=0,
        concat_axis=0,
        tiled=True,
    )
    pieces = pieces.reshape(row_devices, factor, slab_rows, tile_cols * channels)
    pieces = lax.all_to_all(pieces, ROW, split_axis=0, concat_axis=2, tiled=True)
    pieces = pieces.reshape(factor, tile_cols, tile_cols, channels)
    return jnp.transpose(pieces, (0, 2, 1, 3)).reshape(factor * tile_cols, tile_cols, channels)


def on_device(pair_rep, ln_gain, ln_bias, w_in, w_out, w_pde, labels, pair_mask):
    tile_rows, tile_cols, channels = pair_rep.shape
    stride_rows = group_rows(tile_rows, tile_cols)
    blocks = pair_rep.reshape(tile_rows // stride_rows, stride_rows * tile_cols, channels)

    def forward(rows_block):
        return transition(rows_block, ln_gain, ln_bias, w_in, w_out)

    updated = lax.map(forward, blocks).reshape(tile_rows, tile_cols, channels)
    mask_float = pair_mask.astype(jnp.float32)
    local_count = jnp.sum(mask_float)
    valid_count = over_axes(local_count, ROW_COL)
    inverse_count = 1.0 / valid_count
    projected = jnp.einsum("ijc,cb->ijb", updated, w_pde, precision=lax.Precision.HIGHEST)
    scores = projected + mirror(projected)
    highest = jnp.max(scores, axis=-1, keepdims=True)
    shifted = jnp.exp(scores - highest)
    exp_total = jnp.sum(shifted, axis=-1, keepdims=True)
    log_total = highest + jnp.log(exp_total)
    bin_index = lax.broadcasted_iota(jnp.int32, (1, 1, scores.shape[2]), 2)
    onehot = (labels[:, :, None] == bin_index).astype(jnp.float32)
    picked = jnp.sum(scores * onehot, axis=-1, keepdims=True)
    local_loss = jnp.sum(mask_float * (log_total - picked)[:, :, 0])
    d_scores = mask_float[:, :, None] * (shifted / exp_total - onehot) * inverse_count
    d_sym = d_scores + mirror(d_scores)
    d_updated = jnp.einsum("ijb,cb->ijc", d_sym, w_pde, precision=lax.Precision.HIGHEST)
    grad_pde = jnp.einsum("ijc,ijb->cb", updated, d_sym, precision=lax.Precision.HIGHEST)
    cot_blocks = d_updated.reshape(blocks.shape)

    def backward(totals, pieces):
        rows_block, cotangent = pieces
        outcome, pullback = jax.vjp(transition, rows_block, ln_gain, ln_bias, w_in, w_out)
        gradients = pullback(cotangent)
        merged = tuple((earlier + later for earlier, later in zip(totals, gradients[1:])))
        return (merged, gradients[0])

    start_sums = (
        jnp.zeros_like(ln_gain),
        jnp.zeros_like(ln_bias),
        jnp.zeros_like(w_in),
        jnp.zeros_like(w_out),
    )
    param_sums, d_blocks = lax.scan(backward, start_sums, (blocks, cot_blocks))
    g_gain, g_bias, g_in, g_out = param_sums
    row_in, row_out = (sent_and_summed(g_in, ROW, 0), sent_and_summed(g_out, ROW, 0))
    shard_in, shard_out = (sent_and_summed(row_in, COL, 0), sent_and_summed(row_out, COL, 0))
    loss_sum, gain_sum, bias_sum, pde_sum = (
        over_axes(local_loss, ROW_COL),
        over_axes(g_gain, ROW_COL),
        over_axes(g_bias, ROW_COL),
        over_axes(grad_pde, ROW_COL),
    )
    late_scale = 1.0
    mean_loss = loss_sum / valid_count
    d_pair_rep = d_blocks.reshape(pair_rep.shape) * late_scale
    return (
        mean_loss,
        d_pair_rep,
        gain_sum * late_scale,
        bias_sum * late_scale,
        shard_in * late_scale,
        shard_out * late_scale,
        pde_sum * late_scale,
    )


def solution(mesh):
    torus = Mesh(mesh.devices.reshape(2, 4, 8, 2, 2), ("row_0", "row_1", "col_0", "col_1", "col_2"))
    return jax.shard_map(
        on_device,
        mesh=torus,
        in_specs=(P(ROW, COL, None), P(), P(), P(), P(), P(), P(ROW, COL), P(ROW, COL)),
        out_specs=(P(), P(ROW, COL, None), P(), P(), P(ROW_COL, None), P(ROW_COL, None), P()),
        check_vma=False,
    )
```

profile of v0, /device:TPU:1, one launch (start us, length us, event | category | flops | bytes accessed | tf_op | source)
XLA Modules:
  0.0 250.9 jit_solution(8225384277171636121)
XLA Ops:
  0.7 1.1 reduce_sum.162
  1.8 0.1 div.52
  1.9 0.2 multiply_reduce_fusion.2
  2.1 0.6 fusion.37
  2.8 0.5 copy-done.11
  3.3 0.1 copy-done.13
  3.5 1.0 fusion.18
  4.5 0.7 fusion
  5.2 0.1 copy-done.6
  5.3 0.3 fusion.34
  5.5 0.4 copy-done.4
  5.9 0.1 reshape.147
  6.1 10.9 %all_to_all.96 = f32[4,8,1,512]{3,0,2,1:T(4,128)S(1)} all-to-all(f32[4,8,1,512]{3,0,2,1:T(4,128)S(1)} %copy.66), channel_id=1, replica_groups=mesh['row_0'=2,'row_1'=4,'col_0'=8,'col_1'=2,'col_2'=2] {'row_0','row_1'}, dimensions={1} | all-to-all | bytes 131072 | tf_op jit(solution)/shard_map/all_to_all | solution.py:71
  16.9 0.1 all_to_all.69
  17.0 22.7 %all_to_all.97 = f32[32,1,1,512]{3,2,1,0:T(1,128)S(1)} all-to-all(f32[32,1,1,512]{3,2,1,0:T(1,128)S(1)} %bitcast.101), channel_id=1, replica_groups=mesh['row_0'=2,'row_1'=4,'col_0'=8,'col_1'=2,'col_2'=2] {'col_0','col_1'..., dimensions={0} | all-to-all | bytes 131072 | tf_op jit(solution)/shard_map/all_to_all | solution.py:70
  39.7 0.6 copy.68
  40.3 3.5 %all-to-all-start.2 = ((f32[8,4,1,512]{3,1,2,0:T(4,128)}), f32[8,4,1,512]{3,1,2,0:T(4,128)S(1)}, u32[]{:S(2)}, u32[]{:S(2)}) async-start(f32[8,4,1,512]{3,1,2,0:T(4,128)} %copy.68), calls=%async_computation.2 | async-start | bytes 131072 | tf_op jit(solution)/shard_map/all_to_all | solution.py:78
  43.9 0.6 copy-done.16
  44.6 4.4 %all-to-all-done.2 = f32[8,4,1,512]{3,1,2,0:T(4,128)S(1)} async-done(((f32[8,4,1,512]{3,1,2,0:T(4,128)}), f32[8,4,1,512]{3,1,2,0:T(4,128)S(1)}, u32[]{:S(2)}, u32[]{:S(2)}) %all-to-all-start.2) | async-done | bytes 65568 | tf_op jit(solution)/shard_map/all_to_all | solution.py:78
  49.0 0.1 reshape.149
  49.1 0.1 fusion.41
  49.2 0.2 fusion.23
  49.5 0.6 convert_reduce_fusion
  50.1 4.4 %psum.180 = f32[]{:T(128)} all-reduce(f32[]{:T(128)} %get-tuple-element.57), channel_id=1, replica_groups=mesh['row_0'=2,'row_1'=4,'col_0'=8,'col_1'=2,'col_2'=2] {'row_0'}, use_global_device_ids=true, to_apply=%region_12.13 | all-reduce | flops 1 | bytes 8 | tf_op jit(solution)/shard_map/psum | solution.py:17
  54.5 7.6 %psum.181 = f32[]{:T(128)} all-reduce(f32[]{:T(128)} %psum.180), channel_id=1, replica_groups=mesh['row_0'=2,'row_1'=4,'col_0'=8,'col_1'=2,'col_2'=2] {'row_1'}, use_global_device_ids=true, to_apply=%region_13.14 | all-reduce | flops 1 | bytes 8 | tf_op jit(solution)/shard_map/psum | solution.py:17
  62.1 11.7 %psum.182 = f32[]{:T(128)} all-reduce(f32[]{:T(128)} %psum.181), channel_id=1, replica_groups=mesh['row_0'=2,'row_1'=4,'col_0'=8,'col_1'=2,'col_2'=2] {'col_0'}, use_global_device_ids=true, to_apply=%region_14.15 | all-reduce | flops 1 | bytes 8 | tf_op jit(solution)/shard_map/psum | solution.py:17
  73.7 5.9 %psum.183 = f32[]{:T(128)} all-reduce(f32[]{:T(128)} %psum.182), channel_id=1, replica_groups=mesh['row_0'=2,'row_1'=4,'col_0'=8,'col_1'=2,'col_2'=2] {'col_1'}, use_global_device_ids=true, to_apply=%region_15.16 | all-reduce | flops 1 | bytes 8 | tf_op jit(solution)/shard_map/psum | solution.py:17
  79.6 12.7 %psum.184 = f32[]{:T(128)} all-reduce(f32[]{:T(128)} %psum.183), channel_id=1, replica_groups=mesh['row_0'=2,'row_1'=4,'col_0'=8,'col_1'=2,'col_2'=2] {'col_2'}, use_global_device_ids=true, to_apply=%region_16.17 | all-reduce | flops 1 | bytes 8 | tf_op jit(solution)/shard_map/psum | solution.py:17
  93.0 0.2 multiply_multiply_fusion
  93.2 0.1 reshape.151
  93.4 7.6 %all_to_all.98 = f32[4,8,1,512]{3,0,2,1:T(4,128)S(1)} all-to-all(f32[4,8,1,512]{3,0,2,1:T(4,128)S(1)} %copy.72), channel_id=1, replica_groups=mesh['row_0'=2,'row_1'=4,'col_0'=8,'col_1'=2,'col_2'=2] {'row_0','row_1'}, dimensions={1} | all-to-all | bytes 131072 | tf_op jit(solution)/shard_map/all_to_all | solution.py:71
  100.9 0.1 all_to_all.77
  101.0 15.4 %all_to_all.99 = f32[32,1,1,512]{3,2,1,0:T(1,128)S(1)} all-to-all(f32[32,1,1,512]{3,2,1,0:T(1,128)S(1)} %bitcast.104), channel_id=1, replica_groups=mesh['row_0'=2,'row_1'=4,'col_0'=8,'col_1'=2,'col_2'=2] {'col_0','col_1'..., dimensions={0} | all-to-all | bytes 131072 | tf_op jit(solution)/shard_map/all_to_all | solution.py:70
  116.5 7.6 %all_to_all.100 = f32[8,4,1,512]{3,1,2,0:T(4,128)S(1)} all-to-all(f32[8,4,1,512]{3,1,2,0:T(4,128)S(1)} %copy.74), channel_id=1, replica_groups=mesh['row_0'=2,'row_1'=4,'col_0'=8,'col_1'=2,'col_2'=2] {'row_0','row_1'}, dimensions={0} | all-to-all | bytes 131072 | tf_op jit(solution)/shard_map/all_to_all | solution.py:78
  124.2 0.2 bitcast_add_fusion.1
  124.4 0.2 fusion.32
  124.7 0.7 copy-done.20
  125.3 1.6 fusion.38
  126.9 1.4 copy.79
  128.3 1.3 fusion.7
  129.6 4.0 %all-to-all-start.8 = ((f32[8,64,128]{2,1,0:T(8,128)}), f32[8,64,128]{2,1,0:T(8,128)}, u32[]{:S(2)}, u32[]{:S(2)}) async-start(f32[8,64,128]{2,1,0:T(8,128)} %fusion.7), calls=%async_computation.8 | async-start | bytes 524288 | tf_op jit(solution)/shard_map/all_to_all | solution.py:28
  133.8 0.3 copy.81
  134.2 0.6 copy-done.14
  134.8 2.7 %fusion.9 = f32[8,128,128]{2,1,0:T(8,128)} fusion(f32[8,128,256]{2,1,0:T(8,128)S(1)} %bitcast.94, f32[32,8,128]{2,1,0:T(8,128)S(1)} %copy-done.1, f32[128]{0:T(128)S(1)} %copy-done.18, f32[128]{0:T(128)S(1)} %copy-done.14, f32[32,8]{1,0:T(8,128)} %get-tuple-element.98, f32[32,8]{1,0:T(8,128)S(1)} %broadcast_multiply_fusion), kind=kOutput, calls=%fused_computation.16 | convolution fusion | flops 402784256 | bytes 1707008 | tf_op jit(solution)/shard_map/while/body/eval_jaxpr/transpose(jvp())/dot_general | solution.py:37
  137.5 1.1 multiply_reduce_fusion
  138.6 1.6 all-to-all-done.8
  140.1 3.5 %all-to-all-start.6 = ((f32[8,128,128]{2,1,0:T(8,128)}), f32[8,128,128]{2,1,0:T(8,128)S(1)}, u32[]{:S(2)}, u32[]{:S(2)}) async-start(f32[8,128,128]{2,1,0:T(8,128)} %fusion.9), calls=%async_computation.6 | async-start | bytes 1048576 | tf_op jit(solution)/shard_map/all_to_all | solution.py:28
  143.6 0.7 copy-done.12
  144.3 0.3 fusion.40
  144.6 1.6 reduce_sum.174
  146.2 5.5 %all-to-all-done.6 = f32[8,128,128]{2,1,0:T(8,128)S(1)} async-done(((f32[8,128,128]{2,1,0:T(8,128)}), f32[8,128,128]{2,1,0:T(8,128)S(1)}, u32[]{:S(2)}, u32[]{:S(2)}) %all-to-all-start.6) | async-done | bytes 524320 | tf_op jit(solution)/shard_map/all_to_all | solution.py:28
  151.7 6.5 %all-to-all-start.9 = ((f32[32,2,128]{2,1,0:T(2,128)}), f32[32,2,128]{2,1,0:T(2,128)S(1)}, u32[]{:S(2)}, u32[]{:S(2)}) async-start(f32[32,2,128]{2,1,0:T(2,128)} %bitcast.29), calls=%async_computation.9 | async-start | bytes 65536 | tf_op jit(solution)/shard_map/all_to_all | solution.py:28
  158.2 0.4 convolution_bitcast_fusion
  158.6 7.2 %all-reduce.6 = (f32[]{:T(128)}, f32[128]{0:T(128)S(1)}, f32[128]{0:T(128)S(1)}, f32[128,64]{0,1:T(8,128)S(1)}) all-reduce(f32[]{:T(128)} %get-tuple-element.58, f32[128]{0:T(128)S(1)} %get-tuple-element.52, f32[128]{0:T(128)S(1)} %get-tuple-element.54, ...), channel_id=1, replica_groups=mesh['row_0'=2,'row_1'=4,'col_0'=8,'col_1'=2,'col_2'=2] {'row_0'}, use_global_device_ids=true, to_apply=%region_6.7 | all-reduce | flops 8449 | bytes 67592 | tf_op jit(solution)/shard_map/psum | solution.py:17
  165.8 13.7 %all-reduce.3 = (f32[]{:T(128)}, f32[128]{0:T(128)S(1)}, f32[128]{0:T(128)S(1)}, f32[128,64]{0,1:T(8,128)S(1)}) all-reduce(f32[]{:T(128)} %get-tuple-element.87, f32[128]{0:T(128)S(1)} %get-tuple-element.88, f32[128]{0:T(128)S(1)} %get-tuple-element.89, ...), channel_id=1, replica_groups=mesh['row_0'=2,'row_1'=4,'col_0'=8,'col_1'=2,'col_2'=2] {'row_1'}, use_global_device_ids=true, to_apply=%region_7.8 | all-reduce | flops 8449 | bytes 67592 | tf_op jit(solution)/shard_map/psum | solution.py:17
  179.4 23.6 %all-reduce.2 = (f32[]{:T(128)}, f32[128]{0:T(128)S(1)}, f32[128]{0:T(128)S(1)}, f32[128,64]{0,1:T(8,128)S(1)}) all-reduce(f32[]{:T(128)} %get-tuple-element.63, f32[128]{0:T(128)S(1)} %get-tuple-element.76, f32[128]{0:T(128)S(1)} %get-tuple-element.77, ...), channel_id=1, replica_groups=mesh['row_0'=2,'row_1'=4,'col_0'=8,'col_1'=2,'col_2'=2] {'col_0'}, use_global_device_ids=true, to_apply=%region_8.9 | all-reduce | flops 8449 | bytes 67592 | tf_op jit(solution)/shard_map/psum | solution.py:17
  203.1 10.6 %all-reduce.5 = (f32[]{:T(128)}, f32[128]{0:T(128)S(1)}, f32[128]{0:T(128)S(1)}, f32[128,64]{0,1:T(8,128)S(1)}) all-reduce(f32[]{:T(128)} %get-tuple-element.59, f32[128]{0:T(128)S(1)} %get-tuple-element.60, f32[128]{0:T(128)S(1)} %get-tuple-element.61, ...), channel_id=1, replica_groups=mesh['row_0'=2,'row_1'=4,'col_0'=8,'col_1'=2,'col_2'=2] {'col_1'}, use_global_device_ids=true, to_apply=%region_9.10 | all-reduce | flops 8449 | bytes 67592 | tf_op jit(solution)/shard_map/psum | solution.py:17
  213.7 19.8 %all-reduce.4 = (f32[]{:T(128)}, f32[128]{0:T(128)}, f32[128]{0:T(128)}, f32[128,64]{0,1:T(8,128)}) all-reduce(f32[]{:T(128)} %get-tuple-element.83, f32[128]{0:T(128)S(1)} %get-tuple-element.84, f32[128]{0:T(128)S(1)} %get-tuple-element.85, ...), channel_id=1, replica_groups=mesh['row_0'=2,'row_1'=4,'col_0'=8,'col_1'=2,'col_2'=2] {'col_2'}, use_global_device_ids=true, to_apply=%region_10.11 | all-reduce | flops 8449 | bytes 67592 | tf_op jit(solution)/shard_map/psum | solution.py:17
  234.8 0.6 reduce_sum.172
  235.5 3.8 %all-to-all-start.7 = ((f32[32,4,128]{2,1,0:T(4,128)}), f32[32,4,128]{2,1,0:T(4,128)S(1)}, u32[]{:S(2)}, u32[]{:S(2)}) async-start(f32[32,4,128]{2,1,0:T(4,128)} %bitcast.25), calls=%async_computation.7 | async-start | bytes 131072 | tf_op jit(solution)/shard_map/all_to_all | solution.py:28
  239.3 0.8 fusion.14
  240.1 0.6 reduce_sum.175
  240.7 8.5 %all-to-all-done.7 = f32[32,4,128]{2,1,0:T(4,128)S(1)} async-done(((f32[32,4,128]{2,1,0:T(4,128)}), f32[32,4,128]{2,1,0:T(4,128)S(1)}, u32[]{:S(2)}, u32[]{:S(2)}) %all-to-all-start.7) | async-done | bytes 65568 | tf_op jit(solution)/shard_map/all_to_all | solution.py:28
  249.1 0.6 reduce_sum.173
  (52 shorter events, 0.8 us)
Async XLA Ops:
  0.6 2.7 %copy-start = (f32[1024,128]{1,0:T(8,128)S(1)}, f32[1024,128]{1,0:T(8,128)}, u32[]{:S(2)}) copy-start(f32[1024,128]{1,0:T(8,128)} %param.11) | copy-start | bytes 1572868
  0.6 1.2 copy-start.1
  1.9 0.9 copy-start.7
  2.8 0.6 copy-start.11
  2.8 0.7 copy-start.13
  2.8 0.7 copy-start.17
  3.4 1.0 copy-start.9
  3.4 1.0 copy-start.19
  4.5 0.8 copy-start.6
  5.3 0.7 copy-start.4
  40.3 3.5 %copy-start.15 = (s32[32,8]{0,1:T(8,128)S(1)}, s32[32,8]{0,1:T(8,128)}, u32[]{:S(2)}) copy-start(s32[32,8]{0,1:T(8,128)} %param.14) | copy-start | bytes 3076
  40.3 8.6 %all-to-all-start.2 = ((f32[8,4,1,512]{3,1,2,0:T(4,128)}), f32[8,4,1,512]{3,1,2,0:T(4,128)S(1)}, u32[]{:S(2)}, u32[]{:S(2)}) async-start(f32[8,4,1,512]{3,1,2,0:T(4,128)} %copy.68), calls=%async_computation.2 | async-start | bytes 131072 | tf_op jit(solution)/shard_map/all_to_all | solution.py:78
  43.8 0.7 copy-start.16
  124.4 1.0 copy-start.20
  126.9 6.8 %copy-start.2 = (f32[256,512]{1,0:T(8,128)}, f32[256,512]{1,0:T(8,128)S(1)}, u32[]{:S(2)}) copy-start(f32[256,512]{1,0:T(8,128)S(1)} %get-tuple-element.96) | copy-start | bytes 1572868
  129.6 10.5 %all-to-all-start.8 = ((f32[8,64,128]{2,1,0:T(8,128)}), f32[8,64,128]{2,1,0:T(8,128)}, u32[]{:S(2)}, u32[]{:S(2)}) async-start(f32[8,64,128]{2,1,0:T(8,128)} %fusion.7), calls=%async_computation.8 | async-start | bytes 524288 | tf_op jit(solution)/shard_map/all_to_all | solution.py:28
  134.1 0.7 copy-start.14
  134.1 0.7 copy-start.18
  134.8 2.7 %copy-start.3 = (f32[256,512]{1,0:T(8,128)S(1)}, f32[256,512]{1,0:T(8,128)}, u32[]{:S(2)}) copy-start(f32[256,512]{1,0:T(8,128)} %copy-done.2) | copy-start | bytes 1572868
  134.8 2.7 %copy-start.8 = (f32[256]{0:T(256)S(1)}, f32[256]{0:T(256)}, u32[]{:S(2)}) copy-start(f32[256]{0:T(256)} %copy-done.7) | copy-start | bytes 3076
  134.8 2.7 %copy-start.10 = (f32[256]{0:T(256)S(1)}, f32[256]{0:T(256)}, u32[]{:S(2)}) copy-start(f32[256]{0:T(256)} %copy-done.9) | copy-start | bytes 3076
  140.1 11.5 %all-to-all-start.6 = ((f32[8,128,128]{2,1,0:T(8,128)}), f32[8,128,128]{2,1,0:T(8,128)S(1)}, u32[]{:S(2)}, u32[]{:S(2)}) async-start(f32[8,128,128]{2,1,0:T(8,128)} %fusion.9), calls=%async_computation.6 | async-start | bytes 1048576 | tf_op jit(solution)/shard_map/all_to_all | solution.py:28
  143.6 0.7 copy-start.12
  144.6 13.6 %copy-start.5 = (f32[32,8,128]{2,1,0:T(8,128)S(1)}, f32[32,8,128]{2,1,0:T(8,128)}, u32[]{:S(2)}) copy-start(f32[32,8,128]{2,1,0:T(8,128)} %copy-done.4) | copy-start | bytes 393220
  151.7 83.8 %all-to-all-start.9 = ((f32[32,2,128]{2,1,0:T(2,128)}), f32[32,2,128]{2,1,0:T(2,128)S(1)}, u32[]{:S(2)}, u32[]{:S(2)}) async-start(f32[32,2,128]{2,1,0:T(2,128)} %bitcast.29), calls=%async_computation.9 | async-start | bytes 65536 | tf_op jit(solution)/shard_map/all_to_all | solution.py:28
  235.5 13.6 %all-to-all-start.7 = ((f32[32,4,128]{2,1,0:T(4,128)}), f32[32,4,128]{2,1,0:T(4,128)S(1)}, u32[]{:S(2)}, u32[]{:S(2)}) async-start(f32[32,4,128]{2,1,0:T(4,128)} %bitcast.25), calls=%async_computation.7 | async-start | bytes 131072 | tf_op jit(solution)/shard_map/all_to_all | solution.py:28
where the time goes:
time: 252 us; the launch traced here: 251 us
  blocking collectives  181 us (72%)
  starting transfers between devices  21.3 us (8%)
  waiting for transfers between devices  19.9 us (8%)
  matrix products  9.15 us (4%)
  other arithmetic  7.86 us (3%)
  local copies, waits for them, and re-layouts  7.24 us (3%)
  between operations  4.2 us (2%)
    psum x10, blocking collectives, over_axes(): shard = lax.psum(shard, axis)  117 us
    all_to_all x2, blocking collectives, mirror(): lax.all_to_all(lax.all_to_all(pieces, ROW, split_axis=1, concat_axis=0, t...  38.1 us
    all_to_all x2, blocking collectives, mirror(): lax.all_to_all(pieces, ROW, split_axis=1, concat_axis=0, tiled=True)  18.4 us
    all_to_all x4, starting transfers between devices, sent_and_summed(): lax.all_to_all(tiles, axis, split_axis=0, concat_axis=0, tiled=True)  17.8 us
    all_to_all x4, waiting for transfers between devices, sent_and_summed(): lax.all_to_all(tiles, axis, split_axis=0, concat_axis=0, tiled=True)  15.5 us
    all_to_all x1, blocking collectives, mirror(): lax.all_to_all(pieces, ROW, split_axis=0, concat_axis=2, tiled=True)  7.58 us
  transfers between devices with their start and end apart: 5, of which 4 were waited for; matrix products, arithmetic and copies ran while one was open for 3% of the time, Pallas kernels for 0%

commit v1 on v0

v1 whole, which is shorter than its diff:
```python
import functools

import jax
import jax.numpy as jnp
from jax import lax
from jax.experimental import pallas as pl
from jax.experimental.pallas import tpu as pltpu
from jax.sharding import Mesh
from jax.sharding import PartitionSpec as P

AXES = ("yl", "x", "z", "yh", "co")
ROW = ("yl", "x")
COL = ("z", "yh", "co")
PLANE = ("yl", "x", "yh")

EPSILON = 1e-05
ROWS, COLS, C, H, BINS = 32, 8, 128, 512, 64
PAIRS = ROWS * COLS
BIG = 48
SMALL = 40
LABEL, MASK = 64, 65


def split(value):
    high = value.astype(jnp.bfloat16)
    return high, (value - high.astype(jnp.float32)).astype(jnp.bfloat16)


def dot(left, right, left_dim, right_dim):
    dims = (((left_dim,), (right_dim,)), ((), ()))
    one = functools.partial(lax.dot_general, dimension_numbers=dims, preferred_element_type=jnp.float32)
    return one(left[0], right[0]) + (one(left[0], right[1]) + one(left[1], right[0]))


def norm(x, gain, bias):
    centred = x - jnp.mean(x, axis=-1, keepdims=True)
    scale = lax.rsqrt(jnp.mean(centred * centred, axis=-1, keepdims=True) + EPSILON)
    unit = centred * scale
    return scale, unit, unit * gain + bias


def padded(w_pde):
    return jnp.concatenate([w_pde, jnp.zeros((C, C - BINS), jnp.float32)], axis=1)


def forward_kernel(base, x_ref, gain, bias, w_in, w_out, w_pde, labels, mask, send, own, hidden_ref, silu_ref, slope_ref, updated_ref):
    x = x_ref[...]
    _, _, normed = norm(x, gain[...], bias[...])
    projected_in = dot(split(normed), split(w_in[...]), 1, 1)
    gate, up = projected_in[:, :H], projected_in[:, H:]
    sigmoid = 1.0 / (1.0 + jnp.exp(-gate))
    silu = gate * sigmoid
    hidden = silu * up
    silu_ref[...] = silu
    slope_ref[...] = up * (sigmoid * (1.0 + gate * (1.0 - sigmoid)))
    hidden_ref[...] = hidden
    updated = x + dot(split(hidden), split(w_out[...]), 1, 0)
    updated_ref[...] = updated
    projected = dot(split(updated), split(padded(w_pde[...])), 1, 0)
    code = (labels[...] + 64 * mask[...]).astype(jnp.float32).astype(jnp.bfloat16)
    pair = lax.broadcasted_iota(jnp.int32, (PAIRS, ROWS), 0)
    row = lax.broadcasted_iota(jnp.int32, (PAIRS, ROWS), 1)
    spread = jnp.where(pair // COLS == row, 1.0, 0.0).astype(jnp.bfloat16)
    by_row = jnp.dot(spread, code, preferred_element_type=jnp.float32)
    pair = lax.broadcasted_iota(jnp.int32, (PAIRS, COLS), 0)
    col = lax.broadcasted_iota(jnp.int32, (PAIRS, COLS), 1)
    code = jnp.sum(jnp.where(pair % COLS == col, by_row, 0.0), axis=1, keepdims=True)
    scored = jnp.where(code >= 64.0, 1.0, 0.0)
    lane = lax.broadcasted_iota(jnp.int32, (PAIRS, C), 1)
    projected = jnp.where(lane == LABEL, code - 64.0 * scored, projected)
    projected = jnp.where(lane == MASK, scored, projected)
    own[...] = projected
    send[pl.ds(base[0], 4)] = projected.reshape(4, 64, C)
    send[pl.ds(4 - base[0], 4)] = jnp.zeros((4, 64, C), jnp.float32)


def backward_kernel(place, x_ref, gain, bias, w_in, w_out, w_pde, own, received, hidden_ref, silu_ref, slope_ref, updated_ref, send, keep, d_x_ref, mirrored_ref):
    base, core = place[0], place[1]
    for s in range(4):
        for b in range(8):
            mirrored_ref[pl.ds((8 * s + b) * 8, 8), :] = received[base + s, pl.ds(b, 8, stride=8), :]
    mine, mirrored = own[...], mirrored_ref[...]
    lane = lax.broadcasted_iota(jnp.int32, (PAIRS, C), 1)
    lane_float = lane.astype(jnp.float32)
    scored = mine[:, MASK : MASK + 1]
    onehot = lane_float == mine[:, LABEL : LABEL + 1]
    onehot_mirrored = lane_float == mirrored[:, LABEL : LABEL + 1]
    scores = mine + mirrored
    highest = jnp.max(jnp.where(lane < BINS, scores, -jnp.inf), axis=1, keepdims=True)
    shifted = jnp.where(lane < BINS, jnp.exp(jnp.minimum(scores - highest, 0.0)), 0.0)
    total = jnp.sum(shifted, axis=1, keepdims=True)
    picked = jnp.sum(jnp.where(onehot, scores, 0.0), axis=1, keepdims=True)
    loss = jnp.sum(scored * (highest + jnp.log(total) - picked))
    count = jnp.sum(scored)
    labelled = jnp.where(onehot, 1.0, 0.0) + jnp.where(onehot_mirrored, 1.0, 0.0)
    d_sym = scored * (2.0 * (shifted / total) - labelled)
    d_sym = split(d_sym)

    x = x_ref[...]
    scale, unit, normed = norm(x, gain[...], bias[...])
    d_updated = dot(d_sym, split(padded(w_pde[...])), 1, 1)
    d_pde = dot(split(updated_ref[...]), d_sym, 0, 0)
    d_updated_split = split(d_updated)
    d_out = dot(split(hidden_ref[...]), d_updated_split, 0, 0)
    d_hidden = dot(d_updated_split, split(w_out[...]), 1, 1)
    d_in_gate = split(d_hidden * slope_ref[...])
    d_in_up = split(d_hidden * silu_ref[...])
    normed = split(normed)
    d_gate = dot(d_in_gate, normed, 0, 0)
    d_up = dot(d_in_up, normed, 0, 0)
    weights = w_in[...]
    d_normed = dot(d_in_gate, split(weights[:H]), 1, 0) + dot(d_in_up, split(weights[H:]), 1, 0)
    d_unit = d_normed * gain[...]
    d_x_ref[...] = d_updated + scale * (
        d_unit - jnp.mean(d_unit, axis=1, keepdims=True) - unit * jnp.mean(d_unit * unit, axis=1, keepdims=True)
    )

    sub = lax.broadcasted_iota(jnp.int32, (8, C), 0)
    first = core == 0

    def put(rows, lows, highs):
        keep[pl.ds(rows, 8), :] = jnp.where(first, lows, highs)
        send[pl.ds(rows, 8), :] = jnp.where(first, highs, lows)

    for yl, d_half in ((0, d_gate), (1, d_up)):
        for xx in range(4):
            for yh in range(2):
                start = ((yl * 4 + xx) * 2 + yh) * BIG
                for m in range(4):
                    one = (xx * 8 + 2 * m) * 16 + yh * 8
                    even, odd = d_half[one : one + 8], d_half[one + 16 : one + 24]
                    lows = jnp.where(sub < 4, even, pltpu.roll(odd, 4, 0))
                    highs = jnp.where(sub < 4, pltpu.roll(even, 4, 0), odd)
                    put(start + 8 * m, lows, highs)
                for half in range(2):
                    halves = []
                    for cc in range(2):
                        tile = None
                        for low in range(4):
                            one = ((yl * 4 + xx) * 8 + 4 * half + low) * 8
                            shift = (2 * low - 4 * yh - 2 * cc) % 8
                            piece = d_out[one : one + 8]
                            piece = pltpu.roll(piece, shift, 0) if shift else piece
                            tile = piece if low == 0 else jnp.where(sub < 2 * low, tile, piece)
                        halves.append(tile)
                    put(start + 32 + 8 * half, *halves)
    packed = [d_pde[64 * k : 64 * k + 32] + pltpu.roll(d_pde[64 * k + 32 : 64 * k + 64], 64, 1) for k in range(2)]
    for k in range(4):
        put(16 * BIG + 8 * k, packed[0][8 * k : 8 * k + 8], packed[1][8 * k : 8 * k + 8])
    d_gain = jnp.sum(d_normed * unit, axis=0, keepdims=True)
    d_bias = jnp.sum(d_normed, axis=0, keepdims=True)
    lane = lax.broadcasted_iota(jnp.int32, (8, C), 1)
    tail = jnp.where(sub == 0, d_gain, jnp.where(sub == 1, d_bias, 0.0))
    tail = jnp.where((sub == 2) & (lane == 0), loss, tail)
    tail = jnp.where((sub == 2) & (lane == 1), count, tail)
    put(16 * BIG + 32, tail, tail)


def core_sum_kernel(keep, received, send):
    total = keep[...] + received[...]
    for d in range(16):
        send[d, 0:BIG, :] = total[d * BIG : (d + 1) * BIG]
        send[d, BIG : BIG + SMALL, :] = total[16 * BIG :]


def plane_sum_kernel(received, send):
    total = received[0]
    for d in range(1, 16):
        total = total + received[d]
    for z in range(8):
        send[z, 0:4, :] = total[4 * z : 4 * z + 4]
        send[z, 4:6, :] = total[32 + 2 * z : 34 + 2 * z]
        send[z, 6:8, :] = jnp.zeros((2, C), jnp.float32)
        send[z, 8 : 8 + SMALL, :] = total[BIG:]


def column_sum_kernel(received, d_x, loss, d_x_out, d_gain, d_bias, d_in, d_out, d_pde):
    total = received[0]
    for d in range(1, 8):
        total = total + received[d]
    tail = total[40:48]
    count = tail[2:3, 1:2]
    inverse = 1.0 / count
    loss[...] = tail[2:3, 0:1] / count
    d_in[...] = total[0:4] * inverse
    d_out[...] = total[4:6] * inverse
    d_pde[...] = total[8:40] * inverse
    d_gain[...] = tail[0:1] * inverse
    d_bias[...] = tail[1:2] * inverse
    d_x_out[...] = d_x[...] * inverse


def join_kernel(place, mine, other, out):
    core = place[1]
    for who, value in ((core, mine[...]), (1 - core, other[...])):
        out[pl.ds(64 * who, 32), :] = value[:, :BINS]
        out[pl.ds(64 * who + 32, 32), :] = pltpu.roll(value, 64, 1)[:, :BINS]


VMEM = pl.BlockSpec(memory_space=pltpu.VMEM)
SMEM = pl.BlockSpec(memory_space=pltpu.SMEM)


def call(kernel, outs, in_specs, scratch=(), name=None):
    shapes = [jax.ShapeDtypeStruct(shape, jnp.float32) for shape in outs]
    return pl.pallas_call(
        kernel,
        out_shape=shapes,
        in_specs=in_specs,
        out_specs=[VMEM] * len(outs),
        scratch_shapes=list(scratch),
        compiler_params=pltpu.CompilerParams(vmem_limit_bytes=48 << 20),
        name=name,
    )


def mirror_groups():
    groups, diagonal = [], []
    for q in range(8):
        for r in range(q + 1, 8):
            groups.append([q * 32 + 4 * r + u for u in range(4)] + [r * 32 + 4 * q + u for u in range(4)])
        diagonal.append([q * 36 + u for u in range(4)])
    return groups + [diagonal[k] + diagonal[k + 1] for k in range(0, 8, 2)]


def on_device(pair_rep, ln_gain, ln_bias, w_in, w_out, w_pde, labels, pair_mask):
    row, z, core = lax.axis_index(ROW), lax.axis_index("z"), lax.axis_index("co")
    base = jnp.where((row < z) | ((row == z) & (row % 2 == 1)), 4, 0)
    place = jnp.stack([base, core]).astype(jnp.int32)
    x = pair_rep.reshape(PAIRS, C)
    gain, bias = ln_gain.reshape(1, C), ln_bias.reshape(1, C)
    send, own, hidden, silu, slope, updated = call(
        forward_kernel,
        [(8, 64, C), (PAIRS, C), (PAIRS, H), (PAIRS, H), (PAIRS, H), (PAIRS, C)],
        [SMEM] + [VMEM] * 8,
        name="forward",
    )(place, x, gain, bias, w_in, w_out, w_pde, labels, pair_mask)
    received = lax.all_to_all(send, AXES, 0, 0, axis_index_groups=mirror_groups(), tiled=True)
    slab = (16 * BIG + SMALL, C)
    send, keep, d_x = call(
        backward_kernel,
        [slab, slab, (PAIRS, C)],
        [SMEM] + [VMEM] * 12,
        scratch=[pltpu.VMEM((PAIRS, C), jnp.float32)],
        name="backward",
    )(place, x, gain, bias, w_in, w_out, w_pde, own, received, hidden, silu, slope, updated)
    other_core = [(0, 1), (1, 0)]
    received = lax.ppermute(send, "co", other_core)
    (send,) = call(core_sum_kernel, [(16, BIG + SMALL, C)], [VMEM] * 2, name="core_sum")(keep, received)
    received = lax.all_to_all(send, PLANE, 0, 0, tiled=True)
    (send,) = call(plane_sum_kernel, [(8, 8 + SMALL, C)], [VMEM], name="plane_sum")(received)
    received = lax.all_to_all(send, "z", 0, 0, tiled=True)
    loss, d_x, d_gain, d_bias, d_in, d_out, d_pde = call(
        column_sum_kernel,
        [(1, 1), (PAIRS, C), (1, C), (1, C), (4, C), (2, C), (32, C)],
        [VMEM] * 2,
        name="column_sum",
    )(received, d_x)
    other = lax.ppermute(d_pde, "co", other_core)
    (d_pde,) = call(join_kernel, [(C, BINS)], [SMEM] + [VMEM] * 2, name="join")(place, d_pde, other)
    return (
        loss.reshape(()),
        d_x.reshape(ROWS, COLS, C),
        d_gain.reshape(C),
        d_bias.reshape(C),
        d_in,
        d_out,
        d_pde,
    )


def solution(mesh):
    torus = Mesh(mesh.devices.reshape(2, 4, 8, 2, 2), AXES)
    return jax.shard_map(
        on_device,
        mesh=torus,
        in_specs=(P(ROW, COL, None), P(), P(), P(), P(), P(), P(ROW, COL), P(ROW, COL)),
        out_specs=(P(), P(ROW, COL, None), P(), P(), P(ROW + COL, None), P(ROW + COL, None), P()),
        check_vma=False,
    )
```

time: 252 us -> 78.9 us (0.31)
  blocking collectives: 181 us -> 59.3 us
  waiting for transfers between devices: 19.9 us -> 2.22 us
  starting transfers between devices: 21.3 us -> 4.16 us
  matrix products: 9.15 us -> 0 us
  other arithmetic: 7.86 us -> 0.08 us
  Pallas kernels: 0 us -> 6.2 us
  between operations: 4.2 us -> 0.7 us
    psum x10 -> x0, blocking collectives: 117 us -> none  [over_axes(): shard = lax.psum(shard, axis)]
    all_to_all x5 -> x0, starting transfers between devices: 21.3 us -> none  [the longest x4 17.8 us: sent_and_summed(): lax.all_to_all(tiles, axis, split_axis=0, concat_axis=0, tiled=True)]
    all_to_all x5 -> x0, waiting for transfers between devices: 19.9 us -> none  [the longest x4 15.5 us: sent_and_summed(): lax.all_to_all(tiles, axis, split_axis=0, concat_axis=0, tiled=True)]
    dot_general x9 -> x0, matrix products: 9.15 us -> none  [the longest x3 4.76 us: transition(): lax.dot_general(normed, w_in, (((1,), (1,)), ((), ())), precision=lax.Pre...]
    pallas_call x0 -> x6, Pallas kernels: none -> 6.2 us  [the longest x1 2.75 us: on_device(): call(backward_kernel, [slab, slab, (PAIRS, C)], [SMEM] + [VMEM] * 12, scr...]
    reduce_sum x9 -> x0, other arithmetic: 5.86 us -> none  [the longest x4 3.48 us: sent_and_summed(): return arrived.sum(axis=0)]
    all_to_all x5 -> x3, blocking collectives: 64.1 us -> 59.3 us  [the longest x1 27.2 us: on_device(): received = lax.all_to_all(send, PLANE, 0, 0, tiled=True)]
    ppermute x0 -> x2, starting transfers between devices: none -> 4.16 us  [the longest x1 2.98 us: on_device(): other = lax.ppermute(d_pde, 'co', other_core)]
  transfers between devices with their start and end apart: 5 -> 2, of which waited for: 4 -> 2; matrix products, arithmetic and copies ran while one was open for 3% -> 0% of each run, Pallas kernels for 0% -> 0%
where the time goes in v1:
time: 78.9 us; the launch traced here: 78.5 us
  blocking collectives  59.3 us (75%)
  Pallas kernels  6.2 us (8%)
  local copies, waits for them, and re-layouts  5.76 us (7%)
  starting transfers between devices  4.16 us (5%)
  waiting for transfers between devices  2.22 us (3%)
    all_to_all x1, blocking collectives, on_device(): received = lax.all_to_all(send, PLANE, 0, 0, tiled=True)  27.2 us
    all_to_all x1, blocking collectives, on_device(): received = lax.all_to_all(send, 'z', 0, 0, tiled=True)  16.8 us
    all_to_all x1, blocking collectives, on_device(): lax.all_to_all(send, AXES, 0, 0, axis_index_groups=mirror_groups(), tiled...  15.4 us
    unnamed x14, local copies, waits for them, and re-layouts  5.76 us
    ppermute x1, starting transfers between devices, on_device(): other = lax.ppermute(d_pde, 'co', other_core)  2.98 us
    pallas_call x1, Pallas kernels, on_device(): call(backward_kernel, [slab, slab, (PAIRS, C)], [SMEM] + [VMEM] * 12, scr...  2.75 us
    pallas_call x1, Pallas kernels, on_device(): call(forward_kernel, [(8, 64, C), (PAIRS, C), (PAIRS, H), (PAIRS, H), (PA...  1.96 us
  transfers between devices with their start and end apart: 2, of which 2 were waited for; matrix products, arithmetic and copies ran while one was open for 0% of the time, Pallas kernels for 0%

profile of v1, /device:TPU:1, one launch (start us, length us, event | category | flops | bytes accessed | tf_op | source)
XLA Modules:
  0.0 78.5 jit_solution(1239301321406188061)
XLA Ops:
  0.6 0.0 copy-start.2
  0.7 0.8 %copy.16.labels = s32[32,8]{1,0:T(8,128)S(1)} copy(s32[32,8]{0,1:T(8,128)} %param.14) | data formatting | bytes 2048 | tf_op args[6]
  1.5 0.8 copy.17.mask
  2.2 0.8 %copy.18.w_pde = f32[128,64]{1,0:T(8,128)S(1)} copy(f32[128,64]{0,1:T(8,128)} %param.13) | data formatting | bytes 65536 | tf_op args[5]
  3.1 0.1 pad_add_fusion.base.place
  3.2 0.0 copy-start.3
  3.2 0.0 copy-start.4
  3.2 0.0 copy-done.2
  3.2 0.6 copy-done.3
  3.8 0.0 copy-done.4
  3.8 0.0 copy-start
  3.8 1.0 %copy-done = f32[1024,128]{1,0:T(8,128)S(1)} copy-done((f32[1024,128]{1,0:T(8,128)S(1)}, f32[1024,128]{1,0:T(8,128)}, u32[]{:S(2)}) %copy-start) | copy-done | bytes 524312
  4.9 0.0 copy-start.1
  4.9 0.9 %copy-done.1 = f32[512,128]{1,0:T(8,128)S(1)} copy-done((f32[512,128]{1,0:T(8,128)S(1)}, f32[512,128]{1,0:T(8,128)}, u32[]{:S(2)}) %copy-start.1) | copy-done | bytes 262168
  5.8 2.0 %forward.1 = (f32[8,64,128]{2,1,0:T(8,128)S(1)}, f32[256,128]{1,0:T(8,128)S(1)}, f32[256,512]{1,0:T(8,128)S(1)}, f32[256,512]{1,0:T(8,128)S(1)}, f32[256,512]{1,0:T(8,128)S(1)}, /*index=5*/f32[256,128]{1,0:T(8,128)S(1)}) custom-call(s32[2]{0:T(128)S(1)} %pad_add_fusion.base.place, f32[256,128]{1,0:T(8,128)S(1)} %bitcast.9, f32[1,128]{1,0:T(1,128)S(1)} %bitcast.11, ...), custom_call_target="tpu_custom_call" | custom-call | tf_op jit(solution)/shard_map/forward/pallas_call | solution.py:232
  7.8 15.4 %all_to_all.15.received = f32[8,64,128]{2,1,0:T(8,128)S(1)} all-to-all(f32[8,64,128]{2,1,0:T(8,128)S(1)} %get-tuple-element.24), channel_id=1, replica_groups={{4,5,6,7,32,33,34,35},{8,9,10,11,64,65,66,67},{12,13,14,15,96,97,98,99}..., dimensions={0} | all-to-all | bytes 524288 | tf_op jit(solution)/shard_map/all_to_all | solution.py:238
  23.2 2.7 %backward.1 = (f32[808,128]{1,0:T(8,128)S(1)}, f32[808,128]{1,0:T(8,128)S(1)}, f32[256,128]{1,0:T(8,128)S(1)}) custom-call(s32[2]{0:T(128)S(1)} %pad_add_fusion.base.place, f32[256,128]{1,0:T(8,128)S(1)} %bitcast.10, f32[1,128]{1,0:T(1,128)S(1)} %bitcast.12, f32[1,128]{1,0:T(1,128)S(1)} %bitcast.14, f32[1024,128]{1,0:T(8,128)S(1)} %copy-done, ...), custom_call_target="tpu_custom_call" | custom-call | tf_op jit(solution)/shard_map/backward/pallas_call | solution.py:240
  25.9 1.2 %collective-permute-start = (f32[808,128]{1,0:T(8,128)S(1)}, f32[808,128]{1,0:T(8,128)S(1)}, u32[]{:S(2)}, u32[]{:S(2)}) collective-permute-start(f32[808,128]{1,0:T(8,128)S(1)} %get-tuple-element.30), channel_id=1, source_target_pairs={{0,1},{1,0},{2,3},{3,2},{4,5},{5,4},{6,7},{7,6},{8,9},{9,8},{10,11... | collective-permute-start | bytes 1241096 | tf_op jit(solution)/shard_map/ppermute | solution.py:248
  27.1 1.4 %collective-permute-done.received = f32[808,128]{1,0:T(8,128)S(1)} collective-permute-done((f32[808,128]{1,0:T(8,128)S(1)}, f32[808,128]{1,0:T(8,128)S(1)}, u32[]{:S(2)}, u32[]{:S(2)}) %collective-permute-start) | collective-permute-done | bytes 413728 | tf_op jit(solution)/shard_map/ppermute | solution.py:248
  28.5 0.1 core_sum.1
  28.5 27.2 %all_to_all.16.received = f32[16,88,128]{2,1,0:T(8,128)S(1)} all-to-all(f32[16,88,128]{2,1,0:T(8,128)S(1)} %core_sum.1), channel_id=1, replica_groups=mesh['yl'=2,'x'=4,'z'=8,'yh'=2,'co'=2] {'yl','x','yh'}, dimensions={0} | all-to-all | bytes 1441792 | tf_op jit(solution)/shard_map/all_to_all | solution.py:250
  55.8 16.8 %all_to_all.17.received = f32[8,48,128]{2,1,0:T(8,128)S(1)} all-to-all(f32[8,48,128]{2,1,0:T(8,128)S(1)} %plane_sum.1), channel_id=1, replica_groups=mesh['yl'=2,'x'=4,'z'=8,'yh'=2,'co'=2] {'z'}, dimensions={0} | all-to-all | bytes 393216 | tf_op jit(solution)/shard_map/all_to_all | solution.py:252
  72.5 0.8 %column_sum.1 = (f32[1,1]{1,0:T(1,128)}, f32[256,128]{1,0:T(8,128)}, f32[1,128]{1,0:T(1,128)}, f32[1,128]{1,0:T(1,128)}, f32[4,128]{1,0:T(4,128)}, /*index=5*/f32[2,128]{1,0:T(2,128)}, f32[32,128]{1,0:T(8,128)S(1)}) custom-call(f32[8,48,128]{2,1,0:T(8,128)S(1)} %all_to_all.17.received, f32[256,128]{1,0:T(8,128)S(1)} %get-tuple-element.31.d_x), custom_call_target="tpu_custom_call" | custom-call | tf_op jit(solution)/shard_map/column_sum/pallas_call | solution.py:253
  73.3 3.0 %collective-permute-start.1 = (f32[32,128]{1,0:T(8,128)S(1)}, f32[32,128]{1,0:T(8,128)S(1)}, u32[]{:S(2)}, u32[]{:S(2)}) collective-permute-start(f32[32,128]{1,0:T(8,128)S(1)} %get-tuple-element.38.mine), channel_id=1, source_target_pairs={{0,1},{1,0},{2,3},{3,2},{4,5},{5,4},{6,7},{7,6},{8,9},{9,8},{10,11... | collective-permute-start | bytes 49160 | tf_op jit(solution)/shard_map/ppermute | solution.py:259
  76.3 0.8 %collective-permute-done.1.other = f32[32,128]{1,0:T(8,128)S(1)} collective-permute-done((f32[32,128]{1,0:T(8,128)S(1)}, f32[32,128]{1,0:T(8,128)S(1)}, u32[]{:S(2)}, u32[]{:S(2)}) %collective-permute-start.1) | collective-permute-done | bytes 16416 | tf_op jit(solution)/shard_map/ppermute | solution.py:259
  77.2 0.6 join.1
  77.8 0.7 copy.19
  (1 shorter events, 0.0 us)
Async XLA Ops:
  0.6 2.5 %copy-start.2 = (f32[32,8,128]{2,1,0:T(8,128)S(1)}, f32[32,8,128]{2,1,0:T(8,128)}, u32[]{:S(2)}) copy-start(f32[32,8,128]{2,1,0:T(8,128)} %param.8) | copy-start | bytes 393220
  3.2 0.7 copy-start.3
  3.2 0.7 copy-start.4
  3.8 1.0 %copy-start = (f32[1024,128]{1,0:T(8,128)S(1)}, f32[1024,128]{1,0:T(8,128)}, u32[]{:S(2)}) copy-start(f32[1024,128]{1,0:T(8,128)} %w_in.3) | copy-start | bytes 1572868
  4.9 0.9 %copy-start.1 = (f32[512,128]{1,0:T(8,128)S(1)}, f32[512,128]{1,0:T(8,128)}, u32[]{:S(2)}) copy-start(f32[512,128]{1,0:T(8,128)} %w_out.3) | copy-start | bytes 786436
  25.9 2.6 %collective-permute-start = (f32[808,128]{1,0:T(8,128)S(1)}, f32[808,128]{1,0:T(8,128)S(1)}, u32[]{:S(2)}, u32[]{:S(2)}) collective-permute-start(f32[808,128]{1,0:T(8,128)S(1)} %get-tuple-element.30), channel_id=1, source_target_pairs={{0,1},{1,0},{2,3},{3,2},{4,5},{5,4},{6,7},{7,6},{8,9},{9,8},{10,11... | collective-permute-start | bytes 1241096 | tf_op jit(solution)/shard_map/ppermute | solution.py:248
  73.3 3.8 %collective-permute-start.1 = (f32[32,128]{1,0:T(8,128)S(1)}, f32[32,128]{1,0:T(8,128)S(1)}, u32[]{:S(2)}, u32[]{:S(2)}) collective-permute-start(f32[32,128]{1,0:T(8,128)S(1)} %get-tuple-element.38.mine), channel_id=1, source_target_pairs={{0,1},{1,0},{2,3},{3,2},{4,5},{5,4},{6,7},{7,6},{8,9},{9,8},{10,11... | collective-permute-start | bytes 49160 | tf_op jit(solution)/shard_map/ppermute | solution.py:259

commit v2 on v1

v2 whole, which is shorter than its diff:
```python
import functools

import jax
import jax.numpy as jnp
from jax import lax
from jax.experimental import pallas as pl
from jax.experimental.pallas import tpu as pltpu
from jax.sharding import Mesh
from jax.sharding import PartitionSpec as P

AXES = ("yl", "x", "z", "yh", "co")
ROW = ("yl", "x")
COL = ("z", "yh", "co")
PLANE = ("yl", "x", "yh")

EPSILON = 1e-05
ROWS, COLS, C, H, BINS = 32, 8, 128, 512, 64
PAIRS = ROWS * COLS
F32, BF16 = jnp.float32, jnp.bfloat16
LAST = BINS - 1
MASK = BINS
BIG = 40
SMALL = 40
SLAB = 16 * BIG + SMALL


def split(value):
    high = value.astype(jnp.bfloat16)
    return high, (value - high.astype(jnp.float32)).astype(jnp.bfloat16)


def dot(left, right, left_dim, right_dim):
    dims = (((left_dim,), (right_dim,)), ((), ()))
    one = functools.partial(lax.dot_general, dimension_numbers=dims, preferred_element_type=jnp.float32)
    return one(left[0], right[0]) + (one(left[0], right[1]) + one(left[1], right[0]))


def norm(x):
    centred = x - jnp.mean(x, axis=-1, keepdims=True)
    scale = lax.rsqrt(jnp.mean(centred * centred, axis=-1, keepdims=True) + EPSILON)
    return scale, centred * scale


def forward_kernel(
    place, x_hbm, gain_hbm, bias_hbm, w_in_hbm, w_out_hbm, w_pde_hbm, labels_hbm, mask_hbm,
    send, own, gain, w_pde, updated_high, updated_low, unit_ref, scale_ref, normed_high, normed_low,
    in_high, in_low, out_high, out_low, silu_ref, slope_ref, hidden_high, hidden_low,
    x_ref, bias, w_in, w_out, labels, mask, sems,
):
    ins = (x_hbm, gain_hbm, bias_hbm, labels_hbm, mask_hbm, w_in_hbm, w_out_hbm, w_pde_hbm)
    refs = (x_ref, gain, bias, labels, mask, w_in, w_out, w_pde)
    copies = [pltpu.make_async_copy(i, r, sems.at[k]) for k, (i, r) in enumerate(zip(ins, refs))]
    for copy in copies:
        copy.start()
    base = place[0]
    for s in range(4):
        send[4 - base + s] = jnp.zeros((32, C), F32)
    for k in range(3):
        copies[k].wait()
    x = x_ref[...]
    scale, unit = norm(x)
    unit_ref[...] = unit
    scale_ref[...] = jnp.broadcast_to(scale, (PAIRS, C))
    normed = split(unit * gain[...] + bias[...])
    normed_high[...], normed_low[...] = normed
    copies[3].wait()
    copies[4].wait()
    code = (labels[...] + 64 * mask[...]).astype(F32).astype(BF16)
    pair = lax.broadcasted_iota(jnp.int32, (PAIRS, ROWS), 0)
    row = lax.broadcasted_iota(jnp.int32, (PAIRS, ROWS), 1)
    spread = jnp.where(pair // COLS == row, 1.0, 0.0).astype(BF16)
    by_row = lax.dot_general(spread, code, (((1,), (1,)), ((), ())), preferred_element_type=F32)
    pair = lax.broadcasted_iota(jnp.int32, (PAIRS, COLS), 0)
    col = lax.broadcasted_iota(jnp.int32, (PAIRS, COLS), 1)
    code = jnp.sum(jnp.where(pair % COLS == col, by_row, 0.0), axis=1, keepdims=True)
    scored = jnp.where(code >= 64.0, 1.0, 0.0)
    copies[5].wait()
    weights = split(w_in[...])
    in_high[...], in_low[...] = weights
    projected_in = dot(normed, weights, 1, 1)
    gate, up = projected_in[:, :H], projected_in[:, H:]
    sigmoid = 1.0 / (1.0 + jnp.exp(-gate))
    silu = gate * sigmoid
    silu_ref[...] = silu
    slope_ref[...] = up * (sigmoid * (1.0 + gate * (1.0 - sigmoid)))
    hidden = split(silu * up)
    hidden_high[...], hidden_low[...] = hidden
    copies[6].wait()
    weights = split(w_out[...])
    out_high[...], out_low[...] = weights
    updated = split(x + dot(hidden, weights, 1, 0))
    updated_high[...], updated_low[...] = updated
    copies[7].wait()
    weights = jnp.concatenate([w_pde[...], jnp.zeros((C - BINS, C), F32)], axis=0)
    projected = dot(updated, split(weights), 1, 1)
    lane = lax.broadcasted_iota(jnp.int32, (PAIRS, C), 1)
    projected = projected - projected[:, LAST:BINS]
    projected = jnp.where(lane < LAST, projected, jnp.where(lane == LAST, code - 64.0 * scored, scored))
    own[...] = projected
    low = lane[:32] < BINS
    for s in range(4):
        one = projected[64 * s : 64 * s + 32]
        two = projected[64 * s + 32 : 64 * s + 64]
        send[base + s] = jnp.where(low, one, pltpu.roll(two, BINS, 1))


def backward_kernel(
    place, received, own, gain, w_pde, updated_high, updated_low, unit_ref, scale_ref, normed_high, normed_low,
    in_high, in_low, out_high, out_low, silu_ref, slope_ref, hidden_high, hidden_low,
    send, keep, d_x_ref, flat_ref, mirrored_ref,
):
    base, core = place[0], place[1]
    for s in range(4):
        block = received[base + s]
        flat_ref[64 * s : 64 * s + 32, :] = block
        flat_ref[64 * s + 32 : 64 * s + 64, :] = pltpu.roll(block, BINS, 1)
    for s in range(4):
        for b in range(8):
            mirrored_ref[(8 * s + b) * 8 : (8 * s + b) * 8 + 8, :] = flat_ref[pl.ds(64 * s + b, 8, stride=8), :]
    mine, mirrored = own[...], mirrored_ref[...]
    lane = lax.broadcasted_iota(jnp.int32, (PAIRS, C), 1)
    lane_float = lane.astype(jnp.float32)
    scored = mine[:, MASK : MASK + 1]
    onehot = lane_float == mine[:, LAST:BINS]
    onehot_mirrored = lane_float == mirrored[:, LAST:BINS]
    scores = jnp.where(lane < LAST, mine + mirrored, jnp.where(lane == LAST, 0.0, -jnp.inf))
    highest = jnp.max(scores, axis=1, keepdims=True)
    shifted = jnp.exp(scores - highest)
    total = jnp.sum(shifted, axis=1, keepdims=True)
    picked = jnp.sum(jnp.where(onehot, scores, 0.0), axis=1, keepdims=True)
    loss = jnp.sum(scored * (highest + jnp.log(total) - picked))
    count = jnp.sum(scored)
    labelled = jnp.where(onehot, 1.0, 0.0) + jnp.where(onehot_mirrored, 1.0, 0.0)
    d_sym = split(scored * (shifted * (2.0 / total) - labelled))
    narrow = tuple(part[:, :BINS] for part in d_sym)

    d_updated = dot(narrow, split(w_pde[...]), 1, 0)
    d_pde = dot(narrow, (updated_high[...], updated_low[...]), 0, 0)
    d_out = dot((hidden_high[...], hidden_low[...]), d_sym, 0, 0)
    d_hidden = dot(split(d_updated), (out_high[...], out_low[...]), 1, 1)
    d_in_gate = split(d_hidden * slope_ref[...])
    d_in_up = split(d_hidden * silu_ref[...])
    normed = normed_high[...], normed_low[...]
    d_gate = dot(d_in_gate, normed, 0, 0)
    d_up = dot(d_in_up, normed, 0, 0)
    d_normed = dot(d_in_gate, (in_high[:H], in_low[:H]), 1, 0) + dot(d_in_up, (in_high[H:], in_low[H:]), 1, 0)
    unit = unit_ref[...]
    d_unit = d_normed * gain[...]
    d_x_ref[...] = d_updated + scale_ref[...] * (
        d_unit - jnp.mean(d_unit, axis=1, keepdims=True) - unit * jnp.mean(d_unit * unit, axis=1, keepdims=True)
    )

    sub = lax.broadcasted_iota(jnp.int32, (8, C), 0)
    lane = lax.broadcasted_iota(jnp.int32, (8, C), 1)
    first = core == 0

    def put(rows, lows, highs):
        keep[rows : rows + 8, :] = jnp.where(first, lows, highs)
        send[rows : rows + 8, :] = jnp.where(first, highs, lows)

    for yl, d_half in ((0, d_gate), (1, d_up)):
        for xx in range(4):
            for yh in range(2):
                start = ((yl * 4 + xx) * 2 + yh) * BIG
                for m in range(4):
                    one = (xx * 8 + 2 * m) * 16 + yh * 8
                    even, odd = d_half[one : one + 8], d_half[one + 16 : one + 24]
                    lows = jnp.where(sub < 4, even, pltpu.roll(odd, 4, 0))
                    highs = jnp.where(sub < 4, pltpu.roll(even, 4, 0), odd)
                    put(start + 8 * m, lows, highs)
                cores = []
                for cc in range(2):
                    halves = []
                    for half in range(2):
                        tile = None
                        for low in range(4):
                            one = ((yl * 4 + xx) * 8 + 4 * half + low) * 8
                            shift = (2 * low - 4 * yh - 2 * cc) % 8
                            piece = d_out[one : one + 8]
                            piece = pltpu.roll(piece, shift, 0) if shift else piece
                            tile = piece if low == 0 else jnp.where(sub < 2 * low, tile, piece)
                        halves.append(tile)
                    cores.append(jnp.where(lane < BINS, halves[0], pltpu.roll(halves[1], BINS, 1)))
                put(start + 32, *cores)
    for k in range(4):
        put(16 * BIG + 8 * k, d_pde[8 * k : 8 * k + 8], d_pde[32 + 8 * k : 40 + 8 * k])
    d_gain = jnp.sum(d_normed * unit, axis=0, keepdims=True)
    d_bias = jnp.sum(d_normed, axis=0, keepdims=True)
    tail = jnp.where(sub == 0, d_gain, jnp.where(sub == 1, d_bias, 0.0))
    tail = jnp.where((sub == 2) & (lane == 0), loss, tail)
    tail = jnp.where((sub == 2) & (lane == 1), count, tail)
    put(16 * BIG + 32, tail, tail)


def core_sum_kernel(keep, received, send):
    total = keep[...] + received[...]
    for d in range(16):
        send[d, 0:BIG, :] = total[d * BIG : (d + 1) * BIG]
        send[d, BIG : BIG + SMALL, :] = total[16 * BIG :]


def plane_sum_kernel(received, send):
    total = received[0]
    for d in range(1, 16):
        total = total + received[d]
    tail = total[BIG + 32 : BIG + 35]
    lane = lax.broadcasted_iota(jnp.int32, (2, C), 1)
    measures = pltpu.roll(jnp.broadcast_to(tail[2:3], (8, C)), BINS, 1)[0:2]
    for z in range(8):
        send[z, 0:4, :] = total[4 * z : 4 * z + 4]
        pair = total[32 + 2 * (z % 4) : 34 + 2 * (z % 4)]
        pair = pltpu.roll(jnp.concatenate([pair] * 4, axis=0), BINS, 1)[0:2] if z >= 4 else pair
        send[z, 4:6, :] = jnp.where(lane < BINS, pair, measures)
        send[z, 6:8, :] = tail[0:2]
        send[z, 8:40, :] = total[BIG : BIG + 32]


def column_sum_kernel(received, w_pde, d_x, d_pde, loss, d_gain, d_bias, d_in, d_out, d_x_out):
    total = received[0]
    for d in range(1, 8):
        total = total + received[d]
    count = total[4:5, BINS + 1 : BINS + 2]
    inverse = 1.0 / count
    loss[...] = total[4:5, BINS : BINS + 1] / count
    d_pde[...] = total[8:40] * inverse
    d_in[...] = total[0:4] * inverse
    d_gain[...] = total[6:7] * inverse
    d_bias[...] = total[7:8] * inverse
    scores_part = split(total[0:8][:, :BINS])
    d_out[...] = dot(scores_part, split(w_pde[...]), 1, 0)[4:6] * inverse
    d_x_out[...] = d_x[...] * inverse


def join_kernel(place, mine, other, out):
    core = place[1]
    first = core == 0
    out[0:32, :] = jnp.where(first, mine[...], other[...])
    out[32:64, :] = jnp.where(first, other[...], mine[...])


VMEM = pl.BlockSpec(memory_space=pltpu.VMEM)
SMEM = pl.BlockSpec(memory_space=pltpu.SMEM)
HBM = pl.BlockSpec(memory_space=pltpu.HBM)


def call(kernel, outs, in_specs, scratch=(), name=None, limit=12):
    outs = [out if isinstance(out[0], tuple) else (out, F32) for out in outs]
    shapes = [jax.ShapeDtypeStruct(*out) for out in outs]
    return pl.pallas_call(
        kernel,
        out_shape=shapes,
        in_specs=in_specs,
        out_specs=[VMEM] * len(outs),
        scratch_shapes=list(scratch),
        compiler_params=pltpu.CompilerParams(vmem_limit_bytes=limit << 20),
        name=name,
    )


def mirror_groups():
    groups, diagonal = [], []
    for q in range(8):
        for r in range(q + 1, 8):
            groups.append([q * 32 + 4 * r + u for u in range(4)] + [r * 32 + 4 * q + u for u in range(4)])
        diagonal.append([q * 36 + u for u in range(4)])
    return groups + [diagonal[k] + diagonal[k + 1] for k in range(0, 8, 2)]


def on_device(pair_rep, ln_gain, ln_bias, w_in, w_out, w_pde, labels, pair_mask):
    row, z, core = lax.axis_index(ROW), lax.axis_index("z"), lax.axis_index("co")
    base = jnp.where((row < z) | ((row == z) & (row % 2 == 1)), 4, 0)
    place = jnp.stack([base, core]).astype(jnp.int32)
    x = pair_rep.reshape(PAIRS, C)
    gain, bias, w_pde = ln_gain.reshape(1, C), ln_bias.reshape(1, C), w_pde.T
    wide, half = (PAIRS, C), (PAIRS, H)
    send, *kept = call(
        forward_kernel,
        [(8, 32, C), wide, (1, C), (BINS, C), (wide, BF16), (wide, BF16), wide, wide, (wide, BF16), (wide, BF16)]
        + [((2 * H, C), BF16)] * 2
        + [((H, C), BF16)] * 2
        + [half, half, (half, BF16), (half, BF16)],
        [SMEM] + [HBM] * 8,
        scratch=[
            pltpu.VMEM(wide, F32),
            pltpu.VMEM((1, C), F32),
            pltpu.VMEM((2 * H, C), F32),
            pltpu.VMEM((H, C), F32),
            pltpu.VMEM((COLS, ROWS), jnp.int32),
            pltpu.VMEM((COLS, ROWS), jnp.int32),
            pltpu.SemaphoreType.DMA((8,)),
        ],
        name="forward",
    )(place, *(pltpu.with_memory_space_constraint(a, pltpu.HBM) for a in (x, gain, bias, w_in, w_out, w_pde, labels.T, pair_mask.T)))
    received = lax.all_to_all(send, AXES, 0, 0, axis_index_groups=mirror_groups(), tiled=True)
    send, keep, d_x = call(
        backward_kernel,
        [(SLAB, C), (SLAB, C), wide],
        [SMEM] + [VMEM] * 18,
        scratch=[pltpu.VMEM(wide, F32)] * 2,
        name="backward",
    )(place, received, *kept)
    other_core = [(0, 1), (1, 0)]
    received = lax.ppermute(send, "co", other_core)
    (send,) = call(core_sum_kernel, [(16, BIG + SMALL, C)], [VMEM] * 2, name="core_sum")(keep, received)
    received = lax.all_to_all(send, PLANE, 0, 0, tiled=True)
    (send,) = call(plane_sum_kernel, [(8, 40, C)], [VMEM], name="plane_sum")(received)
    received = lax.all_to_all(send, "z", 0, 0, tiled=True)
    d_pde, loss, d_gain, d_bias, d_in, d_out, d_x = call(
        column_sum_kernel,
        [(32, C), (1, 1), (1, C), (1, C), (4, C), (2, C), wide],
        [VMEM] * 3,
        name="column_sum",
    )(received, kept[2], d_x)
    other = lax.ppermute(d_pde, "co", other_core)
    (d_pde,) = call(join_kernel, [(BINS, C)], [SMEM] + [VMEM] * 2, name="join")(place, d_pde, other)
    return (
        loss.reshape(()),
        d_x.reshape(ROWS, COLS, C),
        d_gain.reshape(C),
        d_bias.reshape(C),
        d_in,
        d_out,
        d_pde.T,
    )


def solution(mesh):
    torus = Mesh(mesh.devices.reshape(2, 4, 8, 2, 2), AXES)
    return jax.shard_map(
        on_device,
        mesh=torus,
        in_specs=(P(ROW, COL, None), P(), P(), P(), P(), P(), P(ROW, COL), P(ROW, COL)),
        out_specs=(P(), P(ROW, COL, None), P(), P(), P(ROW + COL, None), P(ROW + COL, None), P()),
        check_vma=False,
    )
```

time: 78.9 us -> 68 us (0.86)
  blocking collectives: 59.3 us -> 52.5 us
  local copies, waits for them, and re-layouts: 5.76 us -> 0 us
  Pallas kernels: 6.2 us -> 8.37 us
    unnamed x14 -> x0, local copies, waits for them, and re-layouts: 5.76 us -> none
    all_to_all x1, blocking collectives: 27.2 us -> 21.8 us  [on_device(): received = lax.all_to_all(send, PLANE, 0, 0, tiled=True)]
    pallas_call x5, Pallas kernels: 6.15 us -> 8.3 us  [the longest x1 3.49 us: on_device(): call(forward_kernel, [(8, 32, C), wide, (1, C), (BINS, C), (wide, BF16),...]
where the time goes in v2:
time: 68 us; the launch traced here: 67.8 us
  blocking collectives  52.5 us (77%)
  Pallas kernels  8.37 us (12%)
  starting transfers between devices  4.02 us (6%)
  waiting for transfers between devices  2.12 us (3%)
    all_to_all x1, blocking collectives, on_device(): received = lax.all_to_all(send, PLANE, 0, 0, tiled=True)  21.8 us
    all_to_all x1, blocking collectives, on_device(): received = lax.all_to_all(send, 'z', 0, 0, tiled=True)  16 us
    all_to_all x1, blocking collectives, on_device(): lax.all_to_all(send, AXES, 0, 0, axis_index_groups=mirror_groups(), tiled...  14.7 us
    pallas_call x1, Pallas kernels, on_device(): call(forward_kernel, [(8, 32, C), wide, (1, C), (BINS, C), (wide, BF16),...  3.49 us
    ppermute x1, starting transfers between devices, on_device(): other = lax.ppermute(d_pde, 'co', other_core)  3.01 us
    pallas_call x1, Pallas kernels, on_device(): call(backward_kernel, [(SLAB, C), (SLAB, C), wide], [SMEM] + [VMEM] * 18,...  2.75 us
  transfers between devices with their start and end apart: 2, of which 2 were waited for; matrix products, arithmetic and copies ran while one was open for 0% of the time, Pallas kernels for 0%

profile of v2, /device:TPU:1, one launch (start us, length us, event | category | flops | bytes accessed | tf_op | source)
XLA Modules:
  0.0 67.8 jit_solution(12749322887032997793)
XLA Ops:
  0.7 0.1 pad_add_fusion.place
  0.7 3.5 %forward.1 = (f32[8,32,128]{2,1,0:T(8,128)S(1)}, f32[256,128]{1,0:T(8,128)S(1)}, f32[1,128]{1,0:T(1,128)S(1)}, f32[64,128]{1,0:T(8,128)S(1)}, bf16[256,128]{1,0:...) custom-call(s32[2]{0:T(128)S(1)} %pad_add_fusion.place, ...), custom_call_target="tpu_custom_call" | custom-call | tf_op jit(solution)/shard_map/forward/pallas_call | solution.py:276
  4.2 14.7 %all_to_all.15.received = f32[8,32,128]{2,1,0:T(8,128)S(1)} all-to-all(f32[8,32,128]{2,1,0:T(8,128)S(1)} %get-tuple-element.35), channel_id=1, replica_groups={{4,5,6,7,32,33,34,35},{8,9,10,11,64,65,66,67},{12,13,14,15,96,97,98,99}..., dimensions={0} | all-to-all | bytes 262144 | tf_op jit(solution)/shard_map/all_to_all | solution.py:294
  18.9 2.7 %backward.1 = (f32[680,128]{1,0:T(8,128)S(1)}, f32[680,128]{1,0:T(8,128)S(1)}, f32[256,128]{1,0:T(8,128)S(1)}) custom-call(s32[2]{0:T(128)S(1)} %pad_add_fusion.place, f32[8,32,128]{2,1,0:T(8,128)S(1)} %all_to_all.15.received, f32[256,128]{1,0:T(8,128)S(1)} %get-tuple-element.36.own, f32[1,128]{1,0:T(1,128)S(1)} %get-tuple-element.37.gain, ...), custom_call_target="tpu_custom_call" | custom-call | tf_op jit(solution)/shard_map/backward/pallas_call | solution.py:295
  21.7 1.0 %collective-permute-start = (f32[680,128]{1,0:T(8,128)S(1)}, f32[680,128]{1,0:T(8,128)S(1)}, u32[]{:S(2)}, u32[]{:S(2)}) collective-permute-start(f32[680,128]{1,0:T(8,128)S(1)} %get-tuple-element.54), channel_id=1, source_target_pairs={{0,1},{1,0},{2,3},{3,2},{4,5},{5,4},{6,7},{7,6},{8,9},{9,8},{10,11... | collective-permute-start | bytes 1044488 | tf_op jit(solution)/shard_map/ppermute | solution.py:303
  22.7 1.3 %collective-permute-done.received = f32[680,128]{1,0:T(8,128)S(1)} collective-permute-done((f32[680,128]{1,0:T(8,128)S(1)}, f32[680,128]{1,0:T(8,128)S(1)}, u32[]{:S(2)}, u32[]{:S(2)}) %collective-permute-start) | collective-permute-done | bytes 348192 | tf_op jit(solution)/shard_map/ppermute | solution.py:303
  24.0 0.1 core_sum.1
  24.1 21.8 %all_to_all.16.received = f32[16,80,128]{2,1,0:T(8,128)S(1)} all-to-all(f32[16,80,128]{2,1,0:T(8,128)S(1)} %core_sum.1), channel_id=1, replica_groups=mesh['yl'=2,'x'=4,'z'=8,'yh'=2,'co'=2] {'yl','x','yh'}, dimensions={0} | all-to-all | bytes 1310720 | tf_op jit(solution)/shard_map/all_to_all | solution.py:305
  45.9 0.1 plane_sum.1
  46.0 16.0 %all_to_all.17.received = f32[8,40,128]{2,1,0:T(8,128)S(1)} all-to-all(f32[8,40,128]{2,1,0:T(8,128)S(1)} %plane_sum.1), channel_id=1, replica_groups=mesh['yl'=2,'x'=4,'z'=8,'yh'=2,'co'=2] {'z'}, dimensions={0} | all-to-all | bytes 327680 | tf_op jit(solution)/shard_map/all_to_all | solution.py:307
  62.0 0.8 %column_sum.1 = (f32[32,128]{1,0:T(8,128)S(1)}, f32[1,1]{1,0:T(1,128)}, f32[1,128]{1,0:T(1,128)}, f32[1,128]{1,0:T(1,128)}, f32[4,128]{1,0:T(4,128)}, /*index=5*/f32[2,128]{1,0:T(2,128)}, f32[256,128]{1,0:T(8,128)}) custom-call(f32[8,40,128]{2,1,0:T(8,128)S(1)} %all_to_all.17.received, f32[64,128]{1,0:T(8,128)S(1)} %get-tuple-element.38.w_pde, ...), custom_call_target="tpu_custom_call" | custom-call | tf_op jit(solution)/shard_map/column_sum/pallas_call | solution.py:308
  62.8 3.0 %collective-permute-start.1 = (f32[32,128]{1,0:T(8,128)S(1)}, f32[32,128]{1,0:T(8,128)S(1)}, u32[]{:S(2)}, u32[]{:S(2)}) collective-permute-start(f32[32,128]{1,0:T(8,128)S(1)} %get-tuple-element.62.mine), channel_id=1, source_target_pairs={{0,1},{1,0},{2,3},{3,2},{4,5},{5,4},{6,7},{7,6},{8,9},{9,8},{10,11... | collective-permute-start | bytes 49160 | tf_op jit(solution)/shard_map/ppermute | solution.py:314
  65.8 0.8 %collective-permute-done.1.other = f32[32,128]{1,0:T(8,128)S(1)} collective-permute-done((f32[32,128]{1,0:T(8,128)S(1)}, f32[32,128]{1,0:T(8,128)S(1)}, u32[]{:S(2)}, u32[]{:S(2)}) %collective-permute-start.1) | collective-permute-done | bytes 16416 | tf_op jit(solution)/shard_map/ppermute | solution.py:314
  66.6 1.2 %join.1 = f32[64,128]{1,0:T(8,128)} custom-call(s32[2]{0:T(128)S(1)} %pad_add_fusion.place, f32[32,128]{1,0:T(8,128)S(1)} %get-tuple-element.62.mine, f32[32,128]{1,0:T(8,128)S(1)} %collective-permute-done.1.other), custom_call_target="tpu_custom_call" | custom-call | tf_op jit(solution)/shard_map/join/pallas_call | solution.py:315
Async XLA Ops:
  21.7 2.3 %collective-permute-start = (f32[680,128]{1,0:T(8,128)S(1)}, f32[680,128]{1,0:T(8,128)S(1)}, u32[]{:S(2)}, u32[]{:S(2)}) collective-permute-start(f32[680,128]{1,0:T(8,128)S(1)} %get-tuple-element.54), channel_id=1, source_target_pairs={{0,1},{1,0},{2,3},{3,2},{4,5},{5,4},{6,7},{7,6},{8,9},{9,8},{10,11... | collective-permute-start | bytes 1044488 | tf_op jit(solution)/shard_map/ppermute | solution.py:303
  62.8 3.9 %collective-permute-start.1 = (f32[32,128]{1,0:T(8,128)S(1)}, f32[32,128]{1,0:T(8,128)S(1)}, u32[]{:S(2)}, u32[]{:S(2)}) collective-permute-start(f32[32,128]{1,0:T(8,128)S(1)} %get-tuple-element.62.mine), channel_id=1, source_target_pairs={{0,1},{1,0},{2,3},{3,2},{4,5},{5,4},{6,7},{7,6},{8,9},{9,8},{10,11... | collective-permute-start | bytes 49160 | tf_op jit(solution)/shard_map/ppermute | solution.py:314

commit v3 on v2

--- a/solution.py
+++ b/solution.py
@@ -29,10 +29,19 @@
     return high, (value - high.astype(jnp.float32)).astype(jnp.bfloat16)
 
 
-def dot(left, right, left_dim, right_dim):
+def product(left, right, left_dim, right_dim):
     dims = (((left_dim,), (right_dim,)), ((), ()))
-    one = functools.partial(lax.dot_general, dimension_numbers=dims, preferred_element_type=jnp.float32)
-    return one(left[0], right[0]) + (one(left[0], right[1]) + one(left[1], right[0]))
+    return lax.dot_general(left, right, dims, preferred_element_type=F32)
+
+
+def wide(left, right, left_dim, right_dim):
+    both = product(left[0], jnp.concatenate(right, axis=1 - right_dim), left_dim, right_dim)
+    return both[:, :C] + (both[:, C:] + product(left[1], right[0], left_dim, right_dim))
+
+
+def deep(left, right, right_dim):
+    stacked = product(jnp.concatenate(left, axis=1), jnp.concatenate([right[0]] * 2, axis=right_dim), 1, right_dim)
+    return stacked + product(left[0], right[1], 1, right_dim)
 
 
 def norm(x):
@@ -41,8 +50,13 @@
     return scale, centred * scale
 
 
+def mirror_base():
+    row, z = lax.axis_index("yl") * 4 + lax.axis_index("x"), lax.axis_index("z")
+    return jnp.where((row < z) | ((row == z) & (row % 2 == 1)), 4, 0)
+
+
 def forward_kernel(
-    place, x_hbm, gain_hbm, bias_hbm, w_in_hbm, w_out_hbm, w_pde_hbm, labels_hbm, mask_hbm,
+    x_hbm, gain_hbm, bias_hbm, w_in_hbm, w_out_hbm, w_pde_hbm, labels_hbm, mask_hbm,
     send, own, gain, w_pde, updated_high, updated_low, unit_ref, scale_ref, normed_high, normed_low,
     in_high, in_low, out_high, out_low, silu_ref, slope_ref, hidden_high, hidden_low,
     x_ref, bias, w_in, w_out, labels, mask, sems,
@@ -52,7 +66,7 @@
     copies = [pltpu.make_async_copy(i, r, sems.at[k]) for k, (i, r) in enumerate(zip(ins, refs))]
     for copy in copies:
         copy.start()
-    base = place[0]
+    base = mirror_base()
     for s in range(4):
         send[4 - base + s] = jnp.zeros((32, C), F32)
     for k in range(3):
@@ -77,7 +91,7 @@
     copies[5].wait()
     weights = split(w_in[...])
     in_high[...], in_low[...] = weights
-    projected_in = dot(normed, weights, 1, 1)
+    projected_in = deep(normed, weights, 1)
     gate, up = projected_in[:, :H], projected_in[:, H:]
     sigmoid = 1.0 / (1.0 + jnp.exp(-gate))
     silu = gate * sigmoid
@@ -88,11 +102,15 @@
     copies[6].wait()
     weights = split(w_out[...])
     out_high[...], out_low[...] = weights
-    updated = split(x + dot(hidden, weights, 1, 0))
+    updated = split(x + wide(hidden, weights, 1, 0))
     updated_high[...], updated_low[...] = updated
     copies[7].wait()
-    weights = jnp.concatenate([w_pde[...], jnp.zeros((C - BINS, C), F32)], axis=0)
-    projected = dot(updated, split(weights), 1, 1)
+    high, low = split(w_pde[...])
+    weights = jnp.concatenate(
+        [jnp.concatenate([high, high], axis=1), jnp.concatenate([low, jnp.zeros_like(low)], axis=1)], axis=0
+    )
+    projected = product(jnp.concatenate(updated, axis=1), weights, 1, 1)
+    projected = projected + pltpu.roll(projected, BINS, 1)
     lane = lax.broadcasted_iota(jnp.int32, (PAIRS, C), 1)
     projected = projected - projected[:, LAST:BINS]
     projected = jnp.where(lane < LAST, projected, jnp.where(lane == LAST, code - 64.0 * scored, scored))
@@ -105,11 +123,11 @@
 
 
 def backward_kernel(
-    place, received, own, gain, w_pde, updated_high, updated_low, unit_ref, scale_ref, normed_high, normed_low,
+    received, own, gain, w_pde, updated_high, updated_low, unit_ref, scale_ref, normed_high, normed_low,
     in_high, in_low, out_high, out_low, silu_ref, slope_ref, hidden_high, hidden_low,
     send, keep, d_x_ref, flat_ref, mirrored_ref,
 ):
-    base, core = place[0], place[1]
+    base, core = mirror_base(), lax.axis_index("co")
     for s in range(4):
         block = received[base + s]
         flat_ref[64 * s : 64 * s + 32, :] = block
@@ -131,19 +149,25 @@
     loss = jnp.sum(scored * (highest + jnp.log(total) - picked))
     count = jnp.sum(scored)
     labelled = jnp.where(onehot, 1.0, 0.0) + jnp.where(onehot_mirrored, 1.0, 0.0)
-    d_sym = split(scored * (shifted * (2.0 / total) - labelled))
-    narrow = tuple(part[:, :BINS] for part in d_sym)
-
-    d_updated = dot(narrow, split(w_pde[...]), 1, 0)
-    d_pde = dot(narrow, (updated_high[...], updated_low[...]), 0, 0)
-    d_out = dot((hidden_high[...], hidden_low[...]), d_sym, 0, 0)
-    d_hidden = dot(split(d_updated), (out_high[...], out_low[...]), 1, 1)
+    d_sym = scored * (shifted * (2.0 / total) - labelled)
+    high = d_sym.astype(BF16)
+    rest = d_sym - high.astype(F32)
+    packed = jnp.where(lane < BINS, high.astype(F32), pltpu.roll(rest, BINS, 1)).astype(BF16)
+
+    high_pde, low_pde = split(w_pde[...])
+    weights = jnp.concatenate([high_pde, high_pde, low_pde, jnp.zeros_like(low_pde)], axis=0)
+    d_updated = product(jnp.concatenate([packed, high], axis=1), weights, 1, 0)
+    d_pde = product(packed, jnp.concatenate([updated_high[...], updated_low[...]], axis=1), 0, 0)
+    d_pde = d_pde[:BINS, :C] + (d_pde[:BINS, C:] + d_pde[BINS:, :C])
+    d_out = product(hidden_high[...], packed, 0, 0)
+    d_out = d_out + (pltpu.roll(d_out, BINS, 1) + product(hidden_low[...], high, 0, 0))
+    d_hidden = deep(split(d_updated), (out_high[...], out_low[...]), 1)
     d_in_gate = split(d_hidden * slope_ref[...])
     d_in_up = split(d_hidden * silu_ref[...])
     normed = normed_high[...], normed_low[...]
-    d_gate = dot(d_in_gate, normed, 0, 0)
-    d_up = dot(d_in_up, normed, 0, 0)
-    d_normed = dot(d_in_gate, (in_high[:H], in_low[:H]), 1, 0) + dot(d_in_up, (in_high[H:], in_low[H:]), 1, 0)
+    d_gate = wide(d_in_gate, normed, 0, 0)
+    d_up = wide(d_in_up, normed, 0, 0)
+    d_normed = wide(d_in_gate, (in_high[:H], in_low[:H]), 1, 0) + wide(d_in_up, (in_high[H:], in_low[H:]), 1, 0)
     unit = unit_ref[...]
     d_unit = d_normed * gain[...]
     d_x_ref[...] = d_updated + scale_ref[...] * (
@@ -215,31 +239,36 @@
         send[z, 8:40, :] = total[BIG : BIG + 32]
 
 
-def column_sum_kernel(received, w_pde, d_x, d_pde, loss, d_gain, d_bias, d_in, d_out, d_x_out):
+def pde_sum_kernel(received, d_pde):
     total = received[0]
     for d in range(1, 8):
         total = total + received[d]
+    d_pde[...] = total[8:40] * (1.0 / total[4:5, BINS + 1 : BINS + 2])
+
+
+def column_sum_kernel(received, w_pde, d_x, loss, d_gain, d_bias, d_in, d_out, d_x_out):
+    total = received[0, 0:8]
+    for d in range(1, 8):
+        total = total + received[d, 0:8]
     count = total[4:5, BINS + 1 : BINS + 2]
     inverse = 1.0 / count
     loss[...] = total[4:5, BINS : BINS + 1] / count
-    d_pde[...] = total[8:40] * inverse
     d_in[...] = total[0:4] * inverse
     d_gain[...] = total[6:7] * inverse
     d_bias[...] = total[7:8] * inverse
-    scores_part = split(total[0:8][:, :BINS])
-    d_out[...] = dot(scores_part, split(w_pde[...]), 1, 0)[4:6] * inverse
+    left, right = split(total[:, :BINS]), split(w_pde[...])
+    projected = product(left[0], right[0], 1, 0) + (product(left[0], right[1], 1, 0) + product(left[1], right[0], 1, 0))
+    d_out[...] = projected[4:6] * inverse
     d_x_out[...] = d_x[...] * inverse
 
 
-def join_kernel(place, mine, other, out):
-    core = place[1]
-    first = core == 0
+def join_kernel(mine, other, out):
+    first = lax.axis_index("co") == 0
     out[0:32, :] = jnp.where(first, mine[...], other[...])
     out[32:64, :] = jnp.where(first, other[...], mine[...])
 
 
 VMEM = pl.BlockSpec(memory_space=pltpu.VMEM)
-SMEM = pl.BlockSpec(memory_space=pltpu.SMEM)
 HBM = pl.BlockSpec(memory_space=pltpu.HBM)
 
 
@@ -267,21 +296,18 @@
 
 
 def on_device(pair_rep, ln_gain, ln_bias, w_in, w_out, w_pde, labels, pair_mask):
-    row, z, core = lax.axis_index(ROW), lax.axis_index("z"), lax.axis_index("co")
-    base = jnp.where((row < z) | ((row == z) & (row % 2 == 1)), 4, 0)
-    place = jnp.stack([base, core]).astype(jnp.int32)
     x = pair_rep.reshape(PAIRS, C)
     gain, bias, w_pde = ln_gain.reshape(1, C), ln_bias.reshape(1, C), w_pde.T
-    wide, half = (PAIRS, C), (PAIRS, H)
+    full, half = (PAIRS, C), (PAIRS, H)
     send, *kept = call(
         forward_kernel,
-        [(8, 32, C), wide, (1, C), (BINS, C), (wide, BF16), (wide, BF16), wide, wide, (wide, BF16), (wide, BF16)]
+        [(8, 32, C), full, (1, C), (BINS, C), (full, BF16), (full, BF16), full, full, (full, BF16), (full, BF16)]
         + [((2 * H, C), BF16)] * 2
         + [((H, C), BF16)] * 2
         + [half, half, (half, BF16), (half, BF16)],
-        [SMEM] + [HBM] * 8,
+        [HBM] * 8,
         scratch=[
-            pltpu.VMEM(wide, F32),
+            pltpu.VMEM(full, F32),
             pltpu.VMEM((1, C), F32),
             pltpu.VMEM((2 * H, C), F32),
             pltpu.VMEM((H, C), F32),
@@ -290,29 +316,30 @@
             pltpu.SemaphoreType.DMA((8,)),
         ],
         name="forward",
-    )(place, *(pltpu.with_memory_space_constraint(a, pltpu.HBM) for a in (x, gain, bias, w_in, w_out, w_pde, labels.T, pair_mask.T)))
+    )(*(pltpu.with_memory_space_constraint(a, pltpu.HBM) for a in (x, gain, bias, w_in, w_out, w_pde, labels.T, pair_mask.T)))
     received = lax.all_to_all(send, AXES, 0, 0, axis_index_groups=mirror_groups(), tiled=True)
     send, keep, d_x = call(
         backward_kernel,
-        [(SLAB, C), (SLAB, C), wide],
-        [SMEM] + [VMEM] * 18,
-        scratch=[pltpu.VMEM(wide, F32)] * 2,
+        [(SLAB, C), (SLAB, C), full],
+        [VMEM] * 18,
+        scratch=[pltpu.VMEM(full, F32)] * 2,
         name="backward",
-    )(place, received, *kept)
+    )(received, *kept)
     other_core = [(0, 1), (1, 0)]
     received = lax.ppermute(send, "co", other_core)
     (send,) = call(core_sum_kernel, [(16, BIG + SMALL, C)], [VMEM] * 2, name="core_sum")(keep, received)
     received = lax.all_to_all(send, PLANE, 0, 0, tiled=True)
     (send,) = call(plane_sum_kernel, [(8, 40, C)], [VMEM], name="plane_sum")(received)
     received = lax.all_to_all(send, "z", 0, 0, tiled=True)
-    d_pde, loss, d_gain, d_bias, d_in, d_out, d_x = call(
+    (d_pde,) = call(pde_sum_kernel, [(32, C)], [VMEM], name="pde_sum")(received)
+    other = lax.ppermute(d_pde, "co", other_core)
+    loss, d_gain, d_bias, d_in, d_out, d_x = call(
         column_sum_kernel,
-        [(32, C), (1, 1), (1, C), (1, C), (4, C), (2, C), wide],
+        [(1, 1), (1, C), (1, C), (4, C), (2, C), full],
         [VMEM] * 3,
         name="column_sum",
     )(received, kept[2], d_x)
-    other = lax.ppermute(d_pde, "co", other_core)
-    (d_pde,) = call(join_kernel, [(BINS, C)], [SMEM] + [VMEM] * 2, name="join")(place, d_pde, other)
+    (d_pde,) = call(join_kernel, [(BINS, C)], [VMEM] * 2, name="join")(d_pde, other)
     return (
         loss.reshape(()),
         d_x.reshape(ROWS, COLS, C),

time: 68 us -> 65.2 us (0.959)
  Pallas kernels: 8.37 us -> 6.3 us
  waiting for transfers between devices: 2.12 us -> 1.34 us
    pallas_call x4 -> x5, Pallas kernels: 8.19 us -> 6.14 us  [the longest x1 2.76 us: on_device(): call(forward_kernel, [(8, 32, C), full, (1, C), (BINS, C), (full, BF16),...]
    ppermute x1, waiting for transfers between devices: 0.84 us -> 0.05 us  [on_device(): other = lax.ppermute(d_pde, 'co', other_core)]
  transfers between devices with their start and end apart: 2 -> 2, of which waited for: 2 -> 2; matrix products, arithmetic and copies ran while one was open for 0% -> 0% of each run, Pallas kernels for 0% -> 1%
where the time goes in v3:
time: 65.2 us; the launch traced here: 65 us
  blocking collectives  52.6 us (81%)
  Pallas kernels  6.3 us (10%)
  starting transfers between devices  4.11 us (6%)
  waiting for transfers between devices  1.34 us (2%)
  between operations  0.66 us (1%)
    all_to_all x1, blocking collectives, on_device(): received = lax.all_to_all(send, PLANE, 0, 0, tiled=True)  21.8 us
    all_to_all x1, blocking collectives, on_device(): received = lax.all_to_all(send, 'z', 0, 0, tiled=True)  16.1 us
    all_to_all x1, blocking collectives, on_device(): lax.all_to_all(send, AXES, 0, 0, axis_index_groups=mirror_groups(), tiled...  14.7 us
    ppermute x1, starting transfers between devices, on_device(): other = lax.ppermute(d_pde, 'co', other_core)  3.1 us
    pallas_call x1, Pallas kernels, on_device(): call(forward_kernel, [(8, 32, C), full, (1, C), (BINS, C), (full, BF16),...  2.76 us
    pallas_call x1, Pallas kernels, on_device(): call(backward_kernel, [(SLAB, C), (SLAB, C), full], [VMEM] * 18, scratch=...  1.86 us
  transfers between devices with their start and end apart: 2, of which 2 were waited for; matrix products, arithmetic and copies ran while one was open for 0% of the time, Pallas kernels for 1%

profile of v3, /device:TPU:1, one launch (start us, length us, event | category | flops | bytes accessed | tf_op | source)
XLA Modules:
  0.0 65.0 jit_solution(15091631131707847890)
XLA Ops:
  0.6 2.8 %forward.1 = (f32[8,32,128]{2,1,0:T(8,128)S(1)}, f32[256,128]{1,0:T(8,128)S(1)}, f32[1,128]{1,0:T(1,128)S(1)}, f32[64,128]{1,0:T(8,128)S(1)}, bf16[256,128]{1,0:...) custom-call(f32[256,128]{1,0:T(8,128)} %bitcast.11, ...), custom_call_target="tpu_custom_call" | custom-call | tf_op jit(solution)/shard_map/forward/pallas_call | solution.py:302
  3.4 14.7 %all_to_all.15.received = f32[8,32,128]{2,1,0:T(8,128)S(1)} all-to-all(f32[8,32,128]{2,1,0:T(8,128)S(1)} %get-tuple-element.34), channel_id=1, replica_groups={{4,5,6,7,32,33,34,35},{8,9,10,11,64,65,66,67},{12,13,14,15,96,97,98,99}..., dimensions={0} | all-to-all | bytes 262144 | tf_op jit(solution)/shard_map/all_to_all | solution.py:320
  18.1 1.9 %backward.1 = (f32[680,128]{1,0:T(8,128)S(1)}, f32[680,128]{1,0:T(8,128)S(1)}, f32[256,128]{1,0:T(8,128)S(1)}) custom-call(f32[8,32,128]{2,1,0:T(8,128)S(1)} %all_to_all.15.received, f32[256,128]{1,0:T(8,128)S(1)} %get-tuple-element.35.own, f32[1,128]{1,0:T(1,128)S(1)} %get-tuple-element.36.gain, f32[64,128]{1,0:T(8,128)S(1)} %get-tuple-element.37.w_pde, ...), custom_call_target="tpu_custom_call" | custom-call | tf_op jit(solution)/shard_map/backward/pallas_call | solution.py:321
  20.0 1.0 %collective-permute-start = (f32[680,128]{1,0:T(8,128)S(1)}, f32[680,128]{1,0:T(8,128)S(1)}, u32[]{:S(2)}, u32[]{:S(2)}) collective-permute-start(f32[680,128]{1,0:T(8,128)S(1)} %get-tuple-element.53), channel_id=1, source_target_pairs={{0,1},{1,0},{2,3},{3,2},{4,5},{5,4},{6,7},{7,6},{8,9},{9,8},{10,11... | collective-permute-start | bytes 1044488 | tf_op jit(solution)/shard_map/ppermute | solution.py:329
  21.0 1.3 %collective-permute-done.received = f32[680,128]{1,0:T(8,128)S(1)} collective-permute-done((f32[680,128]{1,0:T(8,128)S(1)}, f32[680,128]{1,0:T(8,128)S(1)}, u32[]{:S(2)}, u32[]{:S(2)}) %collective-permute-start) | collective-permute-done | bytes 348192 | tf_op jit(solution)/shard_map/ppermute | solution.py:329
  22.3 0.1 core_sum.1
  22.3 21.8 %all_to_all.16.received = f32[16,80,128]{2,1,0:T(8,128)S(1)} all-to-all(f32[16,80,128]{2,1,0:T(8,128)S(1)} %core_sum.1), channel_id=1, replica_groups=mesh['yl'=2,'x'=4,'z'=8,'yh'=2,'co'=2] {'yl','x','yh'}, dimensions={0} | all-to-all | bytes 1310720 | tf_op jit(solution)/shard_map/all_to_all | solution.py:331
  44.1 0.1 plane_sum.1
  44.2 16.1 %all_to_all.17.received = f32[8,40,128]{2,1,0:T(8,128)S(1)} all-to-all(f32[8,40,128]{2,1,0:T(8,128)S(1)} %plane_sum.1), channel_id=1, replica_groups=mesh['yl'=2,'x'=4,'z'=8,'yh'=2,'co'=2] {'z'}, dimensions={0} | all-to-all | bytes 327680 | tf_op jit(solution)/shard_map/all_to_all | solution.py:333
  60.3 0.1 pde_sum.1.mine
  60.4 3.1 %collective-permute-start.1 = (f32[32,128]{1,0:T(8,128)S(1)}, f32[32,128]{1,0:T(8,128)S(1)}, u32[]{:S(2)}, u32[]{:S(2)}) collective-permute-start(f32[32,128]{1,0:T(8,128)S(1)} %pde_sum.1.mine), channel_id=1, source_target_pairs={{0,1},{1,0},{2,3},{3,2},{4,5},{5,4},{6,7},{7,6},{8,9},{9,8},{10,11... | collective-permute-start | bytes 49160 | tf_op jit(solution)/shard_map/ppermute | solution.py:335
  63.5 0.8 %column_sum.1 = (f32[1,1]{1,0:T(1,128)}, f32[1,128]{1,0:T(1,128)}, f32[1,128]{1,0:T(1,128)}, f32[4,128]{1,0:T(4,128)}, f32[2,128]{1,0:T(2,128)}, /*index=5*/f32[256,128]{1,0:T(8,128)}) custom-call(f32[8,40,128]{2,1,0:T(8,128)S(1)} %all_to_all.17.received, f32[64,128]{1,0:T(8,128)S(1)} %get-tuple-element.37.w_pde, f32[256,128]{1,0:T(8,128)S(1)} %get-tuple-element.54.d_x), custom_call_target="tpu_custom_call" | custom-call | tf_op jit(solution)/shard_map/column_sum/pallas_call | solution.py:336
  64.3 0.1 collective-permute-done.1.other
  64.4 0.6 join.1
Async XLA Ops:
  20.0 2.3 %collective-permute-start = (f32[680,128]{1,0:T(8,128)S(1)}, f32[680,128]{1,0:T(8,128)S(1)}, u32[]{:S(2)}, u32[]{:S(2)}) collective-permute-start(f32[680,128]{1,0:T(8,128)S(1)} %get-tuple-element.53), channel_id=1, source_target_pairs={{0,1},{1,0},{2,3},{3,2},{4,5},{5,4},{6,7},{7,6},{8,9},{9,8},{10,11... | collective-permute-start | bytes 1044488 | tf_op jit(solution)/shard_map/ppermute | solution.py:329
  60.4 3.9 %collective-permute-start.1 = (f32[32,128]{1,0:T(8,128)S(1)}, f32[32,128]{1,0:T(8,128)S(1)}, u32[]{:S(2)}, u32[]{:S(2)}) collective-permute-start(f32[32,128]{1,0:T(8,128)S(1)} %pde_sum.1.mine), channel_id=1, source_target_pairs={{0,1},{1,0},{2,3},{3,2},{4,5},{5,4},{6,7},{7,6},{8,9},{9,8},{10,11... | collective-permute-start | bytes 49160 | tf_op jit(solution)/shard_map/ppermute | solution.py:335

commit v4 on v3

--- a/solution.py
+++ b/solution.py
@@ -16,6 +16,7 @@
 EPSILON = 1e-05
 ROWS, COLS, C, H, BINS = 32, 8, 128, 512, 64
 PAIRS = ROWS * COLS
+HALF = PAIRS // 2
 F32, BF16 = jnp.float32, jnp.bfloat16
 LAST = BINS - 1
 MASK = BINS
@@ -50,48 +51,53 @@
     return scale, centred * scale
 
 
-def mirror_base():
-    row, z = lax.axis_index("yl") * 4 + lax.axis_index("x"), lax.axis_index("z")
-    return jnp.where((row < z) | ((row == z) & (row % 2 == 1)), 4, 0)
+def weights_kernel(w_in_hbm, w_out_hbm, in_high, in_low, out_high, out_low, w_in, w_out, sems):
+    copies = [pltpu.make_async_copy(w_in_hbm, w_in, sems.at[0]), pltpu.make_async_copy(w_out_hbm, w_out, sems.at[1])]
+    for copy in copies:
+        copy.start()
+    copies[0].wait()
+    in_high[...], in_low[...] = split(w_in[...])
+    copies[1].wait()
+    out_high[...], out_low[...] = split(w_out[...])
 
 
 def forward_kernel(
-    x_hbm, gain_hbm, bias_hbm, w_in_hbm, w_out_hbm, w_pde_hbm, labels_hbm, mask_hbm,
+    x_hbm, x_other, labels_other, mask_other, in_high, in_low, out_high, out_low,
+    gain_hbm, bias_hbm, w_pde_hbm, labels_hbm, mask_hbm,
     send, own, gain, w_pde, updated_high, updated_low, unit_ref, scale_ref, normed_high, normed_low,
-    in_high, in_low, out_high, out_low, silu_ref, slope_ref, hidden_high, hidden_low,
-    x_ref, bias, w_in, w_out, labels, mask, sems,
+    silu_ref, slope_ref, hidden_high, hidden_low,
+    x_ref, bias, labels, mask, sems,
 ):
-    ins = (x_hbm, gain_hbm, bias_hbm, labels_hbm, mask_hbm, w_in_hbm, w_out_hbm, w_pde_hbm)
-    refs = (x_ref, gain, bias, labels, mask, w_in, w_out, w_pde)
+    core = lax.axis_index("co")
+    first = core == 0
+    rows = pl.ds(pl.multiple_of(core * HALF, HALF), HALF)
+    ins = (x_hbm.at[rows, :], gain_hbm, bias_hbm, labels_hbm, mask_hbm, w_pde_hbm)
+    refs = (x_ref, gain, bias, labels, mask, w_pde)
     copies = [pltpu.make_async_copy(i, r, sems.at[k]) for k, (i, r) in enumerate(zip(ins, refs))]
     for copy in copies:
         copy.start()
-    base = mirror_base()
-    for s in range(4):
-        send[4 - base + s] = jnp.zeros((32, C), F32)
-    for k in range(3):
-        copies[k].wait()
-    x = x_ref[...]
+    copies[0].wait()
+    mine, other = x_ref[...], x_other[rows, :]
+    x = jnp.concatenate([jnp.where(first, mine, other), jnp.where(first, other, mine)], axis=0)
     scale, unit = norm(x)
     unit_ref[...] = unit
     scale_ref[...] = jnp.broadcast_to(scale, (PAIRS, C))
+    for k in range(1, 6):
+        copies[k].wait()
     normed = split(unit * gain[...] + bias[...])
     normed_high[...], normed_low[...] = normed
-    copies[3].wait()
-    copies[4].wait()
-    code = (labels[...] + 64 * mask[...]).astype(F32).astype(BF16)
-    pair = lax.broadcasted_iota(jnp.int32, (PAIRS, ROWS), 0)
-    row = lax.broadcasted_iota(jnp.int32, (PAIRS, ROWS), 1)
-    spread = jnp.where(pair // COLS == row, 1.0, 0.0).astype(BF16)
-    by_row = lax.dot_general(spread, code, (((1,), (1,)), ((), ())), preferred_element_type=F32)
+    mine = (labels[...] + 64 * mask[...]).astype(F32)
+    other = (labels_other[...] + 64 * mask_other[...]).astype(F32)
+    pair = lax.broadcasted_iota(jnp.int32, (HALF, ROWS), 0)
+    row = lax.broadcasted_iota(jnp.int32, (HALF, ROWS), 1)
+    spread = jnp.where(pair // COLS + 16 * core == row, 1.0, 0.0).astype(BF16)
+    codes = (jnp.where(first, mine, other), jnp.where(first, other, mine))
+    by_row = jnp.concatenate([product(spread, code.astype(BF16), 1, 1) for code in codes], axis=0)
     pair = lax.broadcasted_iota(jnp.int32, (PAIRS, COLS), 0)
     col = lax.broadcasted_iota(jnp.int32, (PAIRS, COLS), 1)
     code = jnp.sum(jnp.where(pair % COLS == col, by_row, 0.0), axis=1, keepdims=True)
     scored = jnp.where(code >= 64.0, 1.0, 0.0)
-    copies[5].wait()
-    weights = split(w_in[...])
-    in_high[...], in_low[...] = weights
-    projected_in = deep(normed, weights, 1)
+    projected_in = deep(normed, (in_high[...], in_low[...]), 1)
     gate, up = projected_in[:, :H], projected_in[:, H:]
     sigmoid = 1.0 / (1.0 + jnp.exp(-gate))
     silu = gate * sigmoid
@@ -99,12 +105,8 @@
     slope_ref[...] = up * (sigmoid * (1.0 + gate * (1.0 - sigmoid)))
     hidden = split(silu * up)
     hidden_high[...], hidden_low[...] = hidden
-    copies[6].wait()
-    weights = split(w_out[...])
-    out_high[...], out_low[...] = weights
-    updated = split(x + wide(hidden, weights, 1, 0))
+    updated = split(x + wide(hidden, (out_high[...], out_low[...]), 1, 0))
     updated_high[...], updated_low[...] = updated
-    copies[7].wait()
     high, low = split(w_pde[...])
     weights = jnp.concatenate(
         [jnp.concatenate([high, high], axis=1), jnp.concatenate([low, jnp.zeros_like(low)], axis=1)], axis=0
@@ -115,26 +117,22 @@
     projected = projected - projected[:, LAST:BINS]
     projected = jnp.where(lane < LAST, projected, jnp.where(lane == LAST, code - 64.0 * scored, scored))
     own[...] = projected
-    low = lane[:32] < BINS
-    for s in range(4):
-        one = projected[64 * s : 64 * s + 32]
-        two = projected[64 * s + 32 : 64 * s + 64]
-        send[base + s] = jnp.where(low, one, pltpu.roll(two, BINS, 1))
+    send[...] = jnp.where(lane[:HALF] < BINS, projected[:HALF], pltpu.roll(projected[HALF:], BINS, 1))
 
 
 def backward_kernel(
-    received, own, gain, w_pde, updated_high, updated_low, unit_ref, scale_ref, normed_high, normed_low,
-    in_high, in_low, out_high, out_low, silu_ref, slope_ref, hidden_high, hidden_low,
+    received, in_high, in_low, out_high, out_low, own, gain, w_pde, updated_high, updated_low, unit_ref, scale_ref,
+    normed_high, normed_low, silu_ref, slope_ref, hidden_high, hidden_low,
     send, keep, d_x_ref, flat_ref, mirrored_ref,
 ):
-    base, core = mirror_base(), lax.axis_index("co")
-    for s in range(4):
-        block = received[base + s]
-        flat_ref[64 * s : 64 * s + 32, :] = block
-        flat_ref[64 * s + 32 : 64 * s + 64, :] = pltpu.roll(block, BINS, 1)
-    for s in range(4):
-        for b in range(8):
-            mirrored_ref[(8 * s + b) * 8 : (8 * s + b) * 8 + 8, :] = flat_ref[pl.ds(64 * s + b, 8, stride=8), :]
+    core = lax.axis_index("co")
+    first = core == 0
+    flat_ref[0:HALF, :] = received[...]
+    flat_ref[HALF:PAIRS, :] = pltpu.roll(received[...], BINS, 1)
+    for half in range(2):
+        for row in range(16):
+            start = HALF * (row // 8) + 64 * half + row % 8
+            mirrored_ref[HALF * half + 8 * row : HALF * half + 8 * row + 8, :] = flat_ref[pl.ds(start, 8, stride=8), :]
     mine, mirrored = own[...], mirrored_ref[...]
     lane = lax.broadcasted_iota(jnp.int32, (PAIRS, C), 1)
     lane_float = lane.astype(jnp.float32)
@@ -170,13 +168,14 @@
     d_normed = wide(d_in_gate, (in_high[:H], in_low[:H]), 1, 0) + wide(d_in_up, (in_high[H:], in_low[H:]), 1, 0)
     unit = unit_ref[...]
     d_unit = d_normed * gain[...]
-    d_x_ref[...] = d_updated + scale_ref[...] * (
+    d_x = d_updated + scale_ref[...] * (
         d_unit - jnp.mean(d_unit, axis=1, keepdims=True) - unit * jnp.mean(d_unit * unit, axis=1, keepdims=True)
     )
 
     sub = lax.broadcasted_iota(jnp.int32, (8, C), 0)
     lane = lax.broadcasted_iota(jnp.int32, (8, C), 1)
-    first = core == 0
+    d_x_ref[...] = jnp.where(first, d_x[:HALF], d_x[HALF:])
+    send[SLAB : SLAB + HALF, :] = jnp.where(first, d_x[HALF:], d_x[:HALF])
 
     def put(rows, lows, highs):
         keep[rows : rows + 8, :] = jnp.where(first, lows, highs)
@@ -217,7 +216,7 @@
 
 
 def core_sum_kernel(keep, received, send):
-    total = keep[...] + received[...]
+    total = keep[...] + received[0:SLAB]
     for d in range(16):
         send[d, 0:BIG, :] = total[d * BIG : (d + 1) * BIG]
         send[d, BIG : BIG + SMALL, :] = total[16 * BIG :]
@@ -246,7 +245,7 @@
     d_pde[...] = total[8:40] * (1.0 / total[4:5, BINS + 1 : BINS + 2])
 
 
-def column_sum_kernel(received, w_pde, d_x, loss, d_gain, d_bias, d_in, d_out, d_x_out):
+def column_sum_kernel(received, w_pde, d_x, d_x_other, loss, d_gain, d_bias, d_in, d_out, d_x_out):
     total = received[0, 0:8]
     for d in range(1, 8):
         total = total + received[d, 0:8]
@@ -259,7 +258,10 @@
     left, right = split(total[:, :BINS]), split(w_pde[...])
     projected = product(left[0], right[0], 1, 0) + (product(left[0], right[1], 1, 0) + product(left[1], right[0], 1, 0))
     d_out[...] = projected[4:6] * inverse
-    d_x_out[...] = d_x[...] * inverse
+    first = lax.axis_index("co") == 0
+    mine, other = d_x[...] * inverse, d_x_other[SLAB : SLAB + HALF] * inverse
+    d_x_out[0:HALF, :] = jnp.where(first, mine, other)
+    d_x_out[HALF:PAIRS, :] = jnp.where(first, other, mine)
 
 
 def join_kernel(mine, other, out):
@@ -286,59 +288,65 @@
     )
 
 
-def mirror_groups():
-    groups, diagonal = [], []
-    for q in range(8):
-        for r in range(q + 1, 8):
-            groups.append([q * 32 + 4 * r + u for u in range(4)] + [r * 32 + 4 * q + u for u in range(4)])
-        diagonal.append([q * 36 + u for u in range(4)])
-    return groups + [diagonal[k] + diagonal[k + 1] for k in range(0, 8, 2)]
+def mirror_pairs():
+    return [
+        (r * 32 + z * 4 + yh * 2 + co, z * 32 + r * 4 + co * 2 + yh)
+        for r in range(8)
+        for z in range(8)
+        for yh in range(2)
+        for co in range(2)
+    ]
 
 
 def on_device(pair_rep, ln_gain, ln_bias, w_in, w_out, w_pde, labels, pair_mask):
+    swap = [(0, 1), (1, 0)]
     x = pair_rep.reshape(PAIRS, C)
-    gain, bias, w_pde = ln_gain.reshape(1, C), ln_bias.reshape(1, C), w_pde.T
+    gain, bias, w_pde, labels, mask = ln_gain.reshape(1, C), ln_bias.reshape(1, C), w_pde.T, labels.T, pair_mask.T
+    x_other, labels_other, mask_other = (lax.ppermute(a, "co", swap) for a in (x, labels, mask))
     full, half = (PAIRS, C), (PAIRS, H)
+    in_hbm = functools.partial(pltpu.with_memory_space_constraint, memory_space=pltpu.HBM)
+    weights = call(
+        weights_kernel,
+        [((2 * H, C), BF16)] * 2 + [((H, C), BF16)] * 2,
+        [HBM] * 2,
+        scratch=[pltpu.VMEM((2 * H, C), F32), pltpu.VMEM((H, C), F32), pltpu.SemaphoreType.DMA((2,))],
+        name="weights",
+    )(in_hbm(w_in), in_hbm(w_out))
     send, *kept = call(
         forward_kernel,
-        [(8, 32, C), full, (1, C), (BINS, C), (full, BF16), (full, BF16), full, full, (full, BF16), (full, BF16)]
-        + [((2 * H, C), BF16)] * 2
-        + [((H, C), BF16)] * 2
+        [(HALF, C), full, (1, C), (BINS, C), (full, BF16), (full, BF16), full, full, (full, BF16), (full, BF16)]
         + [half, half, (half, BF16), (half, BF16)],
-        [HBM] * 8,
+        [HBM] + [VMEM] * 7 + [HBM] * 5,
         scratch=[
-            pltpu.VMEM(full, F32),
+            pltpu.VMEM((HALF, C), F32),
             pltpu.VMEM((1, C), F32),
-            pltpu.VMEM((2 * H, C), F32),
-            pltpu.VMEM((H, C), F32),
             pltpu.VMEM((COLS, ROWS), jnp.int32),
             pltpu.VMEM((COLS, ROWS), jnp.int32),
-            pltpu.SemaphoreType.DMA((8,)),
+            pltpu.SemaphoreType.DMA((6,)),
         ],
         name="forward",
-    )(*(pltpu.with_memory_space_constraint(a, pltpu.HBM) for a in (x, gain, bias, w_in, w_out, w_pde, labels.T, pair_mask.T)))
-    received = lax.all_to_all(send, AXES, 0, 0, axis_index_groups=mirror_groups(), tiled=True)
+    )(in_hbm(x), x_other, labels_other, mask_other, *weights, *(in_hbm(a) for a in (gain, bias, w_pde, labels, mask)))
+    received = lax.ppermute(send, AXES, mirror_pairs())
     send, keep, d_x = call(
         backward_kernel,
-        [(SLAB, C), (SLAB, C), full],
+        [(SLAB + HALF, C), (SLAB, C), (HALF, C)],
         [VMEM] * 18,
         scratch=[pltpu.VMEM(full, F32)] * 2,
         name="backward",
-    )(received, *kept)
-    other_core = [(0, 1), (1, 0)]
-    received = lax.ppermute(send, "co", other_core)
-    (send,) = call(core_sum_kernel, [(16, BIG + SMALL, C)], [VMEM] * 2, name="core_sum")(keep, received)
+    )(received, *weights, *kept)
+    from_core = lax.ppermute(send, "co", swap)
+    (send,) = call(core_sum_kernel, [(16, BIG + SMALL, C)], [VMEM] * 2, name="core_sum")(keep, from_core)
     received = lax.all_to_all(send, PLANE, 0, 0, tiled=True)
     (send,) = call(plane_sum_kernel, [(8, 40, C)], [VMEM], name="plane_sum")(received)
     received = lax.all_to_all(send, "z", 0, 0, tiled=True)
     (d_pde,) = call(pde_sum_kernel, [(32, C)], [VMEM], name="pde_sum")(received)
-    other = lax.ppermute(d_pde, "co", other_core)
+    other = lax.ppermute(d_pde, "co", swap)
     loss, d_gain, d_bias, d_in, d_out, d_x = call(
         column_sum_kernel,
         [(1, 1), (1, C), (1, C), (4, C), (2, C), full],
-        [VMEM] * 3,
+        [VMEM] * 4,
         name="column_sum",
-    )(received, kept[2], d_x)
+    )(received, kept[2], d_x, from_core)
     (d_pde,) = call(join_kernel, [(BINS, C)], [VMEM] * 2, name="join")(d_pde, other)
     return (
         loss.reshape(()),

time: 65.2 us -> 64.2 us (0.985)
  blocking collectives: 52.6 us -> 40.5 us
  starting transfers between devices: 4.11 us -> 9.85 us
  waiting for transfers between devices: 1.34 us -> 5.89 us
    all_to_all x1 -> x0, blocking collectives: 14.7 us -> none  [on_device(): lax.all_to_all(send, AXES, 0, 0, axis_index_groups=mirror_groups(), tiled...]
    ppermute x2 -> x6, starting transfers between devices: 4.11 us -> 9.85 us  [the longest x3 3.92 us: on_device(): lax.ppermute(a, 'co', swap)]
    ppermute x2 -> x6, waiting for transfers between devices: 1.34 us -> 5.89 us  [the longest x1 4.09 us: on_device(): received = lax.ppermute(send, AXES, mirror_pairs())]
    all_to_all x1, blocking collectives: 21.8 us -> 24.4 us  [on_device(): received = lax.all_to_all(send, PLANE, 0, 0, tiled=True)]
    pallas_call x2 -> x3, Pallas kernels: 4.61 us -> 5.22 us  [the longest x1 2.21 us: on_device(): call(forward_kernel, [(HALF, C), full, (1, C), (BINS, C), (full, BF16), (...]
  transfers between devices with their start and end apart: 2 -> 6, of which waited for: 2 -> 3; matrix products, arithmetic and copies ran while one was open for 0% -> 0% of each run, Pallas kernels for 1% -> 3%
where the time goes in v4:
time: 64.2 us; the launch traced here: 63.9 us
  blocking collectives  40.5 us (63%)
  starting transfers between devices  9.85 us (15%)
  Pallas kernels  6.91 us (11%)
  waiting for transfers between devices  5.89 us (9%)
  between operations  0.72 us (1%)
    all_to_all x1, blocking collectives, on_device(): received = lax.all_to_all(send, PLANE, 0, 0, tiled=True)  24.4 us
    all_to_all x1, blocking collectives, on_device(): received = lax.all_to_all(send, 'z', 0, 0, tiled=True)  16.1 us
    ppermute x1, waiting for transfers between devices, on_device(): received = lax.ppermute(send, AXES, mirror_pairs())  4.09 us
    ppermute x3, starting transfers between devices, on_device(): lax.ppermute(a, 'co', swap)  3.92 us
    ppermute x1, starting transfers between devices, on_device(): received = lax.ppermute(send, AXES, mirror_pairs())  2.99 us
    ppermute x1, starting transfers between devices, on_device(): other = lax.ppermute(d_pde, 'co', swap)  2.85 us
    pallas_call x1, Pallas kernels, on_device(): call(forward_kernel, [(HALF, C), full, (1, C), (BINS, C), (full, BF16), (...  2.21 us
    pallas_call x1, Pallas kernels, on_device(): call(backward_kernel, [(SLAB + HALF, C), (SLAB, C), (HALF, C)], [VMEM] *...  1.84 us
  transfers between devices with their start and end apart: 6, of which 3 were waited for; matrix products, arithmetic and copies ran while one was open for 0% of the time, Pallas kernels for 3%

profile of v4, /device:TPU:1, one launch (start us, length us, event | category | flops | bytes accessed | tf_op | source)
XLA Modules:
  0.0 63.9 jit_solution(10102178758714235058)
XLA Ops:
  0.6 0.0 copy-start
  0.6 3.3 %collective-permute-start = (f32[256,128]{1,0:T(8,128)}, f32[256,128]{1,0:T(8,128)S(1)}, u32[]{:S(2)}, u32[]{:S(2)}) collective-permute-start(f32[256,128]{1,0:T(8,128)} %bitcast.11), channel_id=1, source_target_pairs={{0,1},{1,0},{2,3},{3,2},{4,5},{5,4},{6,7},{7,6},{8,9},{9,8},{10,11... | collective-permute-start | bytes 393224 | tf_op jit(solution)/shard_map/ppermute | solution.py:305
  4.0 0.1 collective-permute-start.1
  4.1 0.0 copy-done
  4.1 0.5 collective-permute-start.2
  4.6 1.2 %weights.1 = (bf16[1024,128]{1,0:T(8,128)(2,1)S(1)}, bf16[1024,128]{1,0:T(8,128)(2,1)S(1)}, bf16[512,128]{1,0:T(8,128)(2,1)S(1)}, bf16[512,128]{1,0:T(8,128)(2,1)S(1)}) custom-call(f32[1024,128]{1,0:T(8,128)} %w_in_hbm.1, f32[512,128]{1,0:T(8,128)} %w_out_hbm.1), custom_call_target="tpu_custom_call" | custom-call | tf_op jit(solution)/shard_map/weights/pallas_call | solution.py:308
  5.7 0.0 collective-permute-done.1.labels_other
  5.7 0.0 collective-permute-done.2.mask_other
  5.8 0.0 collective-permute-done.x_other
  5.8 2.2 %forward.1 = (f32[128,128]{1,0:T(8,128)S(1)}, f32[256,128]{1,0:T(8,128)S(1)}, f32[1,128]{1,0:T(1,128)S(1)}, f32[64,128]{1,0:T(8,128)S(1)}, bf16[256,128]{1,0:T(8...) custom-call(f32[256,128]{1,0:T(8,128)} %bitcast.12, ...), custom_call_target="tpu_custom_call" | custom-call | tf_op jit(solution)/shard_map/forward/pallas_call | solution.py:315
  8.0 3.0 %collective-permute-start.3 = (f32[128,128]{1,0:T(8,128)S(1)}, f32[128,128]{1,0:T(8,128)S(1)}, u32[]{:S(2)}, u32[]{:S(2)}) collective-permute-start(f32[128,128]{1,0:T(8,128)S(1)} %get-tuple-element.38), channel_id=1, source_target_pairs={{0,0},{1,2},{2,1},{3,3},{4,32},{5,34},{6,33},{7,35},{8,64},{9,66},... | collective-permute-start | bytes 196616 | tf_op jit(solution)/shard_map/ppermute | solution.py:329
  11.0 4.1 %collective-permute-done.3.received = f32[128,128]{1,0:T(8,128)S(1)} collective-permute-done((f32[128,128]{1,0:T(8,128)S(1)}, f32[128,128]{1,0:T(8,128)S(1)}, u32[]{:S(2)}, u32[]{:S(2)}) %collective-permute-start.3) | collective-permute-done | bytes 65568 | tf_op jit(solution)/shard_map/ppermute | solution.py:329
  15.1 1.8 %backward.1 = (f32[808,128]{1,0:T(8,128)S(1)}, f32[680,128]{1,0:T(8,128)S(1)}, f32[128,128]{1,0:T(8,128)S(1)}) custom-call(f32[128,128]{1,0:T(8,128)S(1)} %collective-permute-done.3.received, bf16[1024,128]{1,0:T(8,128)(2,1)S(1)} %get-tuple-element.34.in_high, bf16[1024,128]{1,0:T(8,128)(2,1)S(1)} %get-tuple-element.35.in_low, ...), custom_call_target="tpu_custom_call" | custom-call | tf_op jit(solution)/shard_map/backward/pallas_call | solution.py:330
  16.9 0.1 collective-permute-start.4
  17.0 1.7 %collective-permute-done.4.received.d_x_other = f32[808,128]{1,0:T(8,128)S(1)} collective-permute-done((f32[808,128]{1,0:T(8,128)S(1)}, f32[808,128]{1,0:T(8,128)S(1)}, u32[]{:S(2)}, u32[]{:S(2)}) %collective-permute-start.4) | collective-permute-done | bytes 413728 | tf_op jit(solution)/shard_map/ppermute | solution.py:337
  18.8 24.4 %all_to_all.10.received = f32[16,80,128]{2,1,0:T(8,128)S(1)} all-to-all(f32[16,80,128]{2,1,0:T(8,128)S(1)} %core_sum.1), channel_id=1, replica_groups=mesh['yl'=2,'x'=4,'z'=8,'yh'=2,'co'=2] {'yl','x','yh'}, dimensions={0} | all-to-all | bytes 1310720 | tf_op jit(solution)/shard_map/all_to_all | solution.py:339
  43.3 0.1 plane_sum.1
  43.4 16.1 %all_to_all.11.received = f32[8,40,128]{2,1,0:T(8,128)S(1)} all-to-all(f32[8,40,128]{2,1,0:T(8,128)S(1)} %plane_sum.1), channel_id=1, replica_groups=mesh['yl'=2,'x'=4,'z'=8,'yh'=2,'co'=2] {'z'}, dimensions={0} | all-to-all | bytes 327680 | tf_op jit(solution)/shard_map/all_to_all | solution.py:341
  59.4 0.1 pde_sum.1.mine
  59.6 2.9 %collective-permute-start.5 = (f32[32,128]{1,0:T(8,128)S(1)}, f32[32,128]{1,0:T(8,128)S(1)}, u32[]{:S(2)}, u32[]{:S(2)}) collective-permute-start(f32[32,128]{1,0:T(8,128)S(1)} %pde_sum.1.mine), channel_id=1, source_target_pairs={{0,1},{1,0},{2,3},{3,2},{4,5},{5,4},{6,7},{7,6},{8,9},{9,8},{10,11... | collective-permute-start | bytes 49160 | tf_op jit(solution)/shard_map/ppermute | solution.py:343
  62.4 0.8 %column_sum.1 = (f32[1,1]{1,0:T(1,128)}, f32[1,128]{1,0:T(1,128)}, f32[1,128]{1,0:T(1,128)}, f32[4,128]{1,0:T(4,128)}, f32[2,128]{1,0:T(2,128)}, /*index=5*/f32[256,128]{1,0:T(8,128)}) custom-call(f32[8,40,128]{2,1,0:T(8,128)S(1)} %all_to_all.11.received, f32[64,128]{1,0:T(8,128)S(1)} %get-tuple-element.41.w_pde, f32[128,128]{1,0:T(8,128)S(1)} %get-tuple-element.54.d_x, ...), custom_call_target="tpu_custom_call" | custom-call | tf_op jit(solution)/shard_map/column_sum/pallas_call | solution.py:344
  63.2 0.1 collective-permute-done.5.other
  63.3 0.6 join.1
  (1 shorter events, 0.0 us)
Async XLA Ops:
  0.6 3.4 %copy-start = (s32[32,8]{0,1:T(8,128)S(1)}, s32[32,8]{0,1:T(8,128)}, u32[]{:S(2)}) copy-start(s32[32,8]{0,1:T(8,128)} %param.15) | copy-start | bytes 3076
  0.6 5.1 %collective-permute-start = (f32[256,128]{1,0:T(8,128)}, f32[256,128]{1,0:T(8,128)S(1)}, u32[]{:S(2)}, u32[]{:S(2)}) collective-permute-start(f32[256,128]{1,0:T(8,128)} %bitcast.11), channel_id=1, source_target_pairs={{0,1},{1,0},{2,3},{3,2},{4,5},{5,4},{6,7},{7,6},{8,9},{9,8},{10,11... | collective-permute-start | bytes 393224 | tf_op jit(solution)/shard_map/ppermute | solution.py:305
  4.0 1.8 %collective-permute-start.1 = (s32[8,32]{1,0:T(8,128)}, s32[8,32]{1,0:T(8,128)S(1)}, u32[]{:S(2)}, u32[]{:S(2)}) collective-permute-start(s32[8,32]{1,0:T(8,128)} %bitcast.15), channel_id=1, source_target_pairs={{0,1},{1,0},{2,3},{3,2},{4,5},{5,4},{6,7},{7,6},{8,9},{9,8},{10,11... | collective-permute-start | bytes 3080 | tf_op jit(solution)/shard_map/ppermute | solution.py:305
  4.1 1.7 %collective-permute-start.2 = (s32[8,32]{1,0:T(8,128)S(1)}, s32[8,32]{1,0:T(8,128)S(1)}, u32[]{:S(2)}, u32[]{:S(2)}) collective-permute-start(s32[8,32]{1,0:T(8,128)S(1)} %bitcast.18), channel_id=1, source_target_pairs={{0,1},{1,0},{2,3},{3,2},{4,5},{5,4},{6,7},{7,6},{8,9},{9,8},{10,11... | collective-permute-start | bytes 3080 | tf_op jit(solution)/shard_map/ppermute | solution.py:305
  8.0 7.1 %collective-permute-start.3 = (f32[128,128]{1,0:T(8,128)S(1)}, f32[128,128]{1,0:T(8,128)S(1)}, u32[]{:S(2)}, u32[]{:S(2)}) collective-permute-start(f32[128,128]{1,0:T(8,128)S(1)} %get-tuple-element.38), channel_id=1, source_target_pairs={{0,0},{1,2},{2,1},{3,3},{4,32},{5,34},{6,33},{7,35},{8,64},{9,66},... | collective-permute-start | bytes 196616 | tf_op jit(solution)/shard_map/ppermute | solution.py:329
  16.9 1.8 %collective-permute-start.4 = (f32[808,128]{1,0:T(8,128)S(1)}, f32[808,128]{1,0:T(8,128)S(1)}, u32[]{:S(2)}, u32[]{:S(2)}) collective-permute-start(f32[808,128]{1,0:T(8,128)S(1)} %get-tuple-element.53), channel_id=1, source_target_pairs={{0,1},{1,0},{2,3},{3,2},{4,5},{5,4},{6,7},{7,6},{8,9},{9,8},{10,11... | collective-permute-start | bytes 1241096 | tf_op jit(solution)/shard_map/ppermute | solution.py:337
  59.6 3.7 %collective-permute-start.5 = (f32[32,128]{1,0:T(8,128)S(1)}, f32[32,128]{1,0:T(8,128)S(1)}, u32[]{:S(2)}, u32[]{:S(2)}) collective-permute-start(f32[32,128]{1,0:T(8,128)S(1)} %pde_sum.1.mine), channel_id=1, source_target_pairs={{0,1},{1,0},{2,3},{3,2},{4,5},{5,4},{6,7},{7,6},{8,9},{9,8},{10,11... | collective-permute-start | bytes 49160 | tf_op jit(solution)/shard_map/ppermute | solution.py:343

commit v5 on v4

--- a/solution.py
+++ b/solution.py
@@ -51,39 +51,37 @@
     return scale, centred * scale
 
 
-def weights_kernel(w_in_hbm, w_out_hbm, in_high, in_low, out_high, out_low, w_in, w_out, sems):
-    copies = [pltpu.make_async_copy(w_in_hbm, w_in, sems.at[0]), pltpu.make_async_copy(w_out_hbm, w_out, sems.at[1])]
+def load_kernel(
+    x_hbm, gain_hbm, bias_hbm, labels_hbm, mask_hbm, w_pde_hbm, w_in_hbm, w_out_hbm,
+    x_ref, gain, bias, labels, mask, w_pde, in_high, in_low, out_high, out_low, w_in, w_out, sems,
+):
+    rows = pl.ds(pl.multiple_of(lax.axis_index("co") * HALF, HALF), HALF)
+    ins = (w_in_hbm, w_out_hbm, x_hbm.at[rows, :], gain_hbm, bias_hbm, labels_hbm, mask_hbm, w_pde_hbm)
+    refs = (w_in, w_out, x_ref, gain, bias, labels, mask, w_pde)
+    copies = [pltpu.make_async_copy(i, r, sems.at[k]) for k, (i, r) in enumerate(zip(ins, refs))]
     for copy in copies:
         copy.start()
     copies[0].wait()
     in_high[...], in_low[...] = split(w_in[...])
     copies[1].wait()
     out_high[...], out_low[...] = split(w_out[...])
+    for copy in copies[2:]:
+        copy.wait()
 
 
 def forward_kernel(
-    x_hbm, x_other, labels_other, mask_other, in_high, in_low, out_high, out_low,
-    gain_hbm, bias_hbm, w_pde_hbm, labels_hbm, mask_hbm,
-    send, own, gain, w_pde, updated_high, updated_low, unit_ref, scale_ref, normed_high, normed_low,
+    x_other, labels_other, mask_other, x_ref, gain, bias, labels, mask, w_pde, in_high, in_low, out_high, out_low,
+    send, own, updated_high, updated_low, unit_ref, scale_ref, normed_high, normed_low,
     silu_ref, slope_ref, hidden_high, hidden_low,
-    x_ref, bias, labels, mask, sems,
 ):
     core = lax.axis_index("co")
     first = core == 0
     rows = pl.ds(pl.multiple_of(core * HALF, HALF), HALF)
-    ins = (x_hbm.at[rows, :], gain_hbm, bias_hbm, labels_hbm, mask_hbm, w_pde_hbm)
-    refs = (x_ref, gain, bias, labels, mask, w_pde)
-    copies = [pltpu.make_async_copy(i, r, sems.at[k]) for k, (i, r) in enumerate(zip(ins, refs))]
-    for copy in copies:
-        copy.start()
-    copies[0].wait()
     mine, other = x_ref[...], x_other[rows, :]
     x = jnp.concatenate([jnp.where(first, mine, other), jnp.where(first, other, mine)], axis=0)
     scale, unit = norm(x)
     unit_ref[...] = unit
     scale_ref[...] = jnp.broadcast_to(scale, (PAIRS, C))
-    for k in range(1, 6):
-        copies[k].wait()
     normed = split(unit * gain[...] + bias[...])
     normed_high[...], normed_low[...] = normed
     mine = (labels[...] + 64 * mask[...]).astype(F32)
@@ -121,7 +119,7 @@
 
 
 def backward_kernel(
-    received, in_high, in_low, out_high, out_low, own, gain, w_pde, updated_high, updated_low, unit_ref, scale_ref,
+    received, gain, w_pde, in_high, in_low, out_high, out_low, own, updated_high, updated_low, unit_ref, scale_ref,
     normed_high, normed_low, silu_ref, slope_ref, hidden_high, hidden_low,
     send, keep, d_x_ref, flat_ref, mirrored_ref,
 ):
@@ -181,6 +179,17 @@
         keep[rows : rows + 8, :] = jnp.where(first, lows, highs)
         send[rows : rows + 8, :] = jnp.where(first, highs, lows)
 
+    d_out_tiles = [
+        [
+            jnp.where(
+                lane < BINS,
+                d_out[(8 * k + low) * 8 : (8 * k + low) * 8 + 8],
+                pltpu.roll(d_out[(8 * k + 4 + low) * 8 : (8 * k + 4 + low) * 8 + 8], BINS, 1),
+            )
+            for low in range(4)
+        ]
+        for k in range(8)
+    ]
     for yl, d_half in ((0, d_gate), (1, d_up)):
         for xx in range(4):
             for yh in range(2):
@@ -193,17 +202,12 @@
                     put(start + 8 * m, lows, highs)
                 cores = []
                 for cc in range(2):
-                    halves = []
-                    for half in range(2):
-                        tile = None
-                        for low in range(4):
-                            one = ((yl * 4 + xx) * 8 + 4 * half + low) * 8
-                            shift = (2 * low - 4 * yh - 2 * cc) % 8
-                            piece = d_out[one : one + 8]
-                            piece = pltpu.roll(piece, shift, 0) if shift else piece
-                            tile = piece if low == 0 else jnp.where(sub < 2 * low, tile, piece)
-                        halves.append(tile)
-                    cores.append(jnp.where(lane < BINS, halves[0], pltpu.roll(halves[1], BINS, 1)))
+                    tile = None
+                    for low, piece in enumerate(d_out_tiles[yl * 4 + xx]):
+                        shift = (2 * low - 4 * yh - 2 * cc) % 8
+                        piece = pltpu.roll(piece, shift, 0) if shift else piece
+                        tile = piece if low == 0 else jnp.where(sub < 2 * low, tile, piece)
+                    cores.append(tile)
                 put(start + 32, *cores)
     for k in range(4):
         put(16 * BIG + 8 * k, d_pde[8 * k : 8 * k + 8], d_pde[32 + 8 * k : 40 + 8 * k])
@@ -305,27 +309,22 @@
     x_other, labels_other, mask_other = (lax.ppermute(a, "co", swap) for a in (x, labels, mask))
     full, half = (PAIRS, C), (PAIRS, H)
     in_hbm = functools.partial(pltpu.with_memory_space_constraint, memory_space=pltpu.HBM)
-    weights = call(
-        weights_kernel,
-        [((2 * H, C), BF16)] * 2 + [((H, C), BF16)] * 2,
-        [HBM] * 2,
-        scratch=[pltpu.VMEM((2 * H, C), F32), pltpu.VMEM((H, C), F32), pltpu.SemaphoreType.DMA((2,))],
-        name="weights",
-    )(in_hbm(w_in), in_hbm(w_out))
+    x, gain, bias, labels, mask, *weights = call(
+        load_kernel,
+        [(HALF, C), (1, C), (1, C), ((COLS, ROWS), jnp.int32), ((COLS, ROWS), jnp.int32), (BINS, C)]
+        + [((2 * H, C), BF16)] * 2
+        + [((H, C), BF16)] * 2,
+        [HBM] * 8,
+        scratch=[pltpu.VMEM((2 * H, C), F32), pltpu.VMEM((H, C), F32), pltpu.SemaphoreType.DMA((8,))],
+        name="load",
+    )(*(in_hbm(a) for a in (x, gain, bias, labels, mask, w_pde, w_in, w_out)))
     send, *kept = call(
         forward_kernel,
-        [(HALF, C), full, (1, C), (BINS, C), (full, BF16), (full, BF16), full, full, (full, BF16), (full, BF16)]
+        [(HALF, C), full, (full, BF16), (full, BF16), full, full, (full, BF16), (full, BF16)]
         + [half, half, (half, BF16), (half, BF16)],
-        [HBM] + [VMEM] * 7 + [HBM] * 5,
-        scratch=[
-            pltpu.VMEM((HALF, C), F32),
-            pltpu.VMEM((1, C), F32),
-            pltpu.VMEM((COLS, ROWS), jnp.int32),
-            pltpu.VMEM((COLS, ROWS), jnp.int32),
-            pltpu.SemaphoreType.DMA((6,)),
-        ],
+        [VMEM] * 13,
         name="forward",
-    )(in_hbm(x), x_other, labels_other, mask_other, *weights, *(in_hbm(a) for a in (gain, bias, w_pde, labels, mask)))
+    )(x_other, labels_other, mask_other, x, gain, bias, labels, mask, *weights)
     received = lax.ppermute(send, AXES, mirror_pairs())
     send, keep, d_x = call(
         backward_kernel,
@@ -333,7 +332,7 @@
         [VMEM] * 18,
         scratch=[pltpu.VMEM(full, F32)] * 2,
         name="backward",
-    )(received, *weights, *kept)
+    )(received, gain, *weights, *kept)
     from_core = lax.ppermute(send, "co", swap)
     (send,) = call(core_sum_kernel, [(16, BIG + SMALL, C)], [VMEM] * 2, name="core_sum")(keep, from_core)
     received = lax.all_to_all(send, PLANE, 0, 0, tiled=True)
@@ -346,7 +345,7 @@
         [(1, 1), (1, C), (1, C), (4, C), (2, C), full],
         [VMEM] * 4,
         name="column_sum",
-    )(received, kept[2], d_x, from_core)
+    )(received, weights[0], d_x, from_core)
     (d_pde,) = call(join_kernel, [(BINS, C)], [VMEM] * 2, name="join")(d_pde, other)
     return (
         loss.reshape(()),

time: 64.2 us -> 63.3 us (0.986)
  Pallas kernels: 6.91 us -> 6.06 us
    pallas_call x2, Pallas kernels: 3.38 us -> 2.53 us  [the longest x1 1.3 us: on_device(): call(forward_kernel, [(HALF, C), full, (full, BF16), (full, BF16), full,...]
where the time goes in v5:
time: 63.3 us; the launch traced here: 63 us
  blocking collectives  40.5 us (64%)
  starting transfers between devices  9.85 us (16%)
  Pallas kernels  6.06 us (10%)
  waiting for transfers between devices  5.89 us (9%)
  between operations  0.72 us (1%)
    all_to_all x1, blocking collectives, on_device(): received = lax.all_to_all(send, PLANE, 0, 0, tiled=True)  24.4 us
    all_to_all x1, blocking collectives, on_device(): received = lax.all_to_all(send, 'z', 0, 0, tiled=True)  16.1 us
    ppermute x1, waiting for transfers between devices, on_device(): received = lax.ppermute(send, AXES, mirror_pairs())  4.09 us
    ppermute x3, starting transfers between devices, on_device(): lax.ppermute(a, 'co', swap)  3.92 us
    ppermute x1, starting transfers between devices, on_device(): received = lax.ppermute(send, AXES, mirror_pairs())  2.99 us
    ppermute x1, starting transfers between devices, on_device(): other = lax.ppermute(d_pde, 'co', swap)  2.85 us
    pallas_call x1, Pallas kernels, on_device(): call(backward_kernel, [(SLAB + HALF, C), (SLAB, C), (HALF, C)], [VMEM] *...  1.85 us
    ppermute x1, waiting for transfers between devices, on_device(): from_core = lax.ppermute(send, 'co', swap)  1.74 us
  transfers between devices with their start and end apart: 6, of which 3 were waited for; matrix products, arithmetic and copies ran while one was open for 0% of the time, Pallas kernels for 3%

profile of v5, /device:TPU:1, one launch (start us, length us, event | category | flops | bytes accessed | tf_op | source)
XLA Modules:
  0.0 63.0 jit_solution(2370519721940420140)
XLA Ops:
  0.6 0.0 copy-start
  0.6 3.3 %collective-permute-start = (f32[256,128]{1,0:T(8,128)}, f32[256,128]{1,0:T(8,128)S(1)}, u32[]{:S(2)}, u32[]{:S(2)}) collective-permute-start(f32[256,128]{1,0:T(8,128)} %bitcast.11), channel_id=1, source_target_pairs={{0,1},{1,0},{2,3},{3,2},{4,5},{5,4},{6,7},{7,6},{8,9},{9,8},{10,11... | collective-permute-start | bytes 393224 | tf_op jit(solution)/shard_map/ppermute | solution.py:309
  4.0 0.1 collective-permute-start.1
  4.1 0.0 copy-done
  4.1 0.5 collective-permute-start.2
  4.6 1.2 %load.1 = (f32[128,128]{1,0:T(8,128)S(1)}, f32[1,128]{1,0:T(1,128)S(1)}, f32[1,128]{1,0:T(1,128)S(1)}, s32[8,32]{1,0:T(8,128)S(1)}, s32[8,32]{1,0:T(8,128)S(1)},...) custom-call(f32[256,128]{1,0:T(8,128)} %bitcast.12, ...), custom_call_target="tpu_custom_call" | custom-call | tf_op jit(solution)/shard_map/load/pallas_call | solution.py:312
  5.8 0.0 collective-permute-done.1.labels_other
  5.8 0.0 collective-permute-done.2.mask_other
  5.8 0.0 collective-permute-done.x_other
  5.8 1.3 %forward.1 = (f32[128,128]{1,0:T(8,128)S(1)}, f32[256,128]{1,0:T(8,128)S(1)}, bf16[256,128]{1,0:T(8,128)(2,1)S(1)}, bf16[256,128]{1,0:T(8,128)(2,1)S(1)}, f32[25...) custom-call(f32[256,128]{1,0:T(8,128)S(1)} %collective-permute-done., ...), custom_call_target="tpu_custom_call" | custom-call | tf_op jit(solution)/shard_map/forward/pallas_call | solution.py:321
  7.1 3.0 %collective-permute-start.3 = (f32[128,128]{1,0:T(8,128)S(1)}, f32[128,128]{1,0:T(8,128)S(1)}, u32[]{:S(2)}, u32[]{:S(2)}) collective-permute-start(f32[128,128]{1,0:T(8,128)S(1)} %get-tuple-element.48), channel_id=1, source_target_pairs={{0,0},{1,2},{2,1},{3,3},{4,32},{5,34},{6,33},{7,35},{8,64},{9,66},... | collective-permute-start | bytes 196616 | tf_op jit(solution)/shard_map/ppermute | solution.py:328
  10.1 4.1 %collective-permute-done.3.received = f32[128,128]{1,0:T(8,128)S(1)} collective-permute-done((f32[128,128]{1,0:T(8,128)S(1)}, f32[128,128]{1,0:T(8,128)S(1)}, u32[]{:S(2)}, u32[]{:S(2)}) %collective-permute-start.3) | collective-permute-done | bytes 65568 | tf_op jit(solution)/shard_map/ppermute | solution.py:328
  14.2 1.8 %backward.1 = (f32[808,128]{1,0:T(8,128)S(1)}, f32[680,128]{1,0:T(8,128)S(1)}, f32[128,128]{1,0:T(8,128)S(1)}) custom-call(f32[128,128]{1,0:T(8,128)S(1)} %collective-permute-done.3.received, f32[1,128]{1,0:T(1,128)S(1)} %get-tuple-element.39.gain, f32[64,128]{1,0:T(8,128)S(1)} %get-tuple-element.43.w_pde, bf16[1024,128]{1,0:T(8,128)(2,1)S(1)} %get-tuple-element.44.in_high, ...), custom_call_target="tpu_custom_call" | custom-call | tf_op jit(solution)/shard_map/backward/pallas_call | solution.py:329
  16.1 0.1 collective-permute-start.4
  16.2 1.7 %collective-permute-done.4.received.d_x_other = f32[808,128]{1,0:T(8,128)S(1)} collective-permute-done((f32[808,128]{1,0:T(8,128)S(1)}, f32[808,128]{1,0:T(8,128)S(1)}, u32[]{:S(2)}, u32[]{:S(2)}) %collective-permute-start.4) | collective-permute-done | bytes 413728 | tf_op jit(solution)/shard_map/ppermute | solution.py:336
  18.0 24.4 %all_to_all.10.received = f32[16,80,128]{2,1,0:T(8,128)S(1)} all-to-all(f32[16,80,128]{2,1,0:T(8,128)S(1)} %core_sum.1), channel_id=1, replica_groups=mesh['yl'=2,'x'=4,'z'=8,'yh'=2,'co'=2] {'yl','x','yh'}, dimensions={0} | all-to-all | bytes 1310720 | tf_op jit(solution)/shard_map/all_to_all | solution.py:338
  42.4 0.1 plane_sum.1
  42.5 16.1 %all_to_all.11.received = f32[8,40,128]{2,1,0:T(8,128)S(1)} all-to-all(f32[8,40,128]{2,1,0:T(8,128)S(1)} %plane_sum.1), channel_id=1, replica_groups=mesh['yl'=2,'x'=4,'z'=8,'yh'=2,'co'=2] {'z'}, dimensions={0} | all-to-all | bytes 327680 | tf_op jit(solution)/shard_map/all_to_all | solution.py:340
  58.6 0.1 pde_sum.1.mine
  58.7 2.9 %collective-permute-start.5 = (f32[32,128]{1,0:T(8,128)S(1)}, f32[32,128]{1,0:T(8,128)S(1)}, u32[]{:S(2)}, u32[]{:S(2)}) collective-permute-start(f32[32,128]{1,0:T(8,128)S(1)} %pde_sum.1.mine), channel_id=1, source_target_pairs={{0,1},{1,0},{2,3},{3,2},{4,5},{5,4},{6,7},{7,6},{8,9},{9,8},{10,11... | collective-permute-start | bytes 49160 | tf_op jit(solution)/shard_map/ppermute | solution.py:342
  61.6 0.8 %column_sum.1 = (f32[1,1]{1,0:T(1,128)}, f32[1,128]{1,0:T(1,128)}, f32[1,128]{1,0:T(1,128)}, f32[4,128]{1,0:T(4,128)}, f32[2,128]{1,0:T(2,128)}, /*index=5*/f32[256,128]{1,0:T(8,128)}) custom-call(f32[8,40,128]{2,1,0:T(8,128)S(1)} %all_to_all.11.received, f32[64,128]{1,0:T(8,128)S(1)} %get-tuple-element.43.w_pde, f32[128,128]{1,0:T(8,128)S(1)} %get-tuple-element.62.d_x, ...), custom_call_target="tpu_custom_call" | custom-call | tf_op jit(solution)/shard_map/column_sum/pallas_call | solution.py:343
  62.4 0.1 collective-permute-done.5.other
  62.4 0.6 join.1
  (1 shorter events, 0.0 us)
Async XLA Ops:
  0.6 3.4 %copy-start = (s32[32,8]{0,1:T(8,128)S(1)}, s32[32,8]{0,1:T(8,128)}, u32[]{:S(2)}) copy-start(s32[32,8]{0,1:T(8,128)} %param.15) | copy-start | bytes 3076
  0.6 5.2 %collective-permute-start = (f32[256,128]{1,0:T(8,128)}, f32[256,128]{1,0:T(8,128)S(1)}, u32[]{:S(2)}, u32[]{:S(2)}) collective-permute-start(f32[256,128]{1,0:T(8,128)} %bitcast.11), channel_id=1, source_target_pairs={{0,1},{1,0},{2,3},{3,2},{4,5},{5,4},{6,7},{7,6},{8,9},{9,8},{10,11... | collective-permute-start | bytes 393224 | tf_op jit(solution)/shard_map/ppermute | solution.py:309
  4.0 1.8 %collective-permute-start.1 = (s32[8,32]{1,0:T(8,128)}, s32[8,32]{1,0:T(8,128)S(1)}, u32[]{:S(2)}, u32[]{:S(2)}) collective-permute-start(s32[8,32]{1,0:T(8,128)} %bitcast.15), channel_id=1, source_target_pairs={{0,1},{1,0},{2,3},{3,2},{4,5},{5,4},{6,7},{7,6},{8,9},{9,8},{10,11... | collective-permute-start | bytes 3080 | tf_op jit(solution)/shard_map/ppermute | solution.py:309
  4.1 1.7 %collective-permute-start.2 = (s32[8,32]{1,0:T(8,128)S(1)}, s32[8,32]{1,0:T(8,128)S(1)}, u32[]{:S(2)}, u32[]{:S(2)}) collective-permute-start(s32[8,32]{1,0:T(8,128)S(1)} %bitcast.18), channel_id=1, source_target_pairs={{0,1},{1,0},{2,3},{3,2},{4,5},{5,4},{6,7},{7,6},{8,9},{9,8},{10,11... | collective-permute-start | bytes 3080 | tf_op jit(solution)/shard_map/ppermute | solution.py:309
  7.1 7.1 %collective-permute-start.3 = (f32[128,128]{1,0:T(8,128)S(1)}, f32[128,128]{1,0:T(8,128)S(1)}, u32[]{:S(2)}, u32[]{:S(2)}) collective-permute-start(f32[128,128]{1,0:T(8,128)S(1)} %get-tuple-element.48), channel_id=1, source_target_pairs={{0,0},{1,2},{2,1},{3,3},{4,32},{5,34},{6,33},{7,35},{8,64},{9,66},... | collective-permute-start | bytes 196616 | tf_op jit(solution)/shard_map/ppermute | solution.py:328
  16.1 1.8 %collective-permute-start.4 = (f32[808,128]{1,0:T(8,128)S(1)}, f32[808,128]{1,0:T(8,128)S(1)}, u32[]{:S(2)}, u32[]{:S(2)}) collective-permute-start(f32[808,128]{1,0:T(8,128)S(1)} %get-tuple-element.61), channel_id=1, source_target_pairs={{0,1},{1,0},{2,3},{3,2},{4,5},{5,4},{6,7},{7,6},{8,9},{9,8},{10,11... | collective-permute-start | bytes 1241096 | tf_op jit(solution)/shard_map/ppermute | solution.py:336
  58.7 3.7 %collective-permute-start.5 = (f32[32,128]{1,0:T(8,128)S(1)}, f32[32,128]{1,0:T(8,128)S(1)}, u32[]{:S(2)}, u32[]{:S(2)}) collective-permute-start(f32[32,128]{1,0:T(8,128)S(1)} %pde_sum.1.mine), channel_id=1, source_target_pairs={{0,1},{1,0},{2,3},{3,2},{4,5},{5,4},{6,7},{7,6},{8,9},{9,8},{10,11... | collective-permute-start | bytes 49160 | tf_op jit(solution)/shard_map/ppermute | solution.py:342

commit v6 on v5

--- a/solution.py
+++ b/solution.py
@@ -53,7 +53,7 @@
 
 def load_kernel(
     x_hbm, gain_hbm, bias_hbm, labels_hbm, mask_hbm, w_pde_hbm, w_in_hbm, w_out_hbm,
-    x_ref, gain, bias, labels, mask, w_pde, in_high, in_low, out_high, out_low, w_in, w_out, sems,
+    x_ref, gain, bias, code, w_pde, in_high, in_low, out_high, out_low, w_in, w_out, labels, mask, sems,
 ):
     rows = pl.ds(pl.multiple_of(lax.axis_index("co") * HALF, HALF), HALF)
     ins = (w_in_hbm, w_out_hbm, x_hbm.at[rows, :], gain_hbm, bias_hbm, labels_hbm, mask_hbm, w_pde_hbm)
@@ -67,11 +67,12 @@
     out_high[...], out_low[...] = split(w_out[...])
     for copy in copies[2:]:
         copy.wait()
+    code[...] = (labels[...] + 64 * mask[...]).astype(F32)
 
 
 def forward_kernel(
-    x_other, labels_other, mask_other, x_ref, gain, bias, labels, mask, w_pde, in_high, in_low, out_high, out_low,
-    send, own, updated_high, updated_low, unit_ref, scale_ref, normed_high, normed_low,
+    x_other, x_ref, gain, bias, w_pde, in_high, in_low, out_high, out_low,
+    scores_ref, updated_high, updated_low, unit_ref, scale_ref, normed_high, normed_low,
     silu_ref, slope_ref, hidden_high, hidden_low,
 ):
     core = lax.axis_index("co")
@@ -84,17 +85,6 @@
     scale_ref[...] = jnp.broadcast_to(scale, (PAIRS, C))
     normed = split(unit * gain[...] + bias[...])
     normed_high[...], normed_low[...] = normed
-    mine = (labels[...] + 64 * mask[...]).astype(F32)
-    other = (labels_other[...] + 64 * mask_other[...]).astype(F32)
-    pair = lax.broadcasted_iota(jnp.int32, (HALF, ROWS), 0)
-    row = lax.broadcasted_iota(jnp.int32, (HALF, ROWS), 1)
-    spread = jnp.where(pair // COLS + 16 * core == row, 1.0, 0.0).astype(BF16)
-    codes = (jnp.where(first, mine, other), jnp.where(first, other, mine))
-    by_row = jnp.concatenate([product(spread, code.astype(BF16), 1, 1) for code in codes], axis=0)
-    pair = lax.broadcasted_iota(jnp.int32, (PAIRS, COLS), 0)
-    col = lax.broadcasted_iota(jnp.int32, (PAIRS, COLS), 1)
-    code = jnp.sum(jnp.where(pair % COLS == col, by_row, 0.0), axis=1, keepdims=True)
-    scored = jnp.where(code >= 64.0, 1.0, 0.0)
     projected_in = deep(normed, (in_high[...], in_low[...]), 1)
     gate, up = projected_in[:, :H], projected_in[:, H:]
     sigmoid = 1.0 / (1.0 + jnp.exp(-gate))
@@ -111,9 +101,24 @@
     )
     projected = product(jnp.concatenate(updated, axis=1), weights, 1, 1)
     projected = projected + pltpu.roll(projected, BINS, 1)
+    scores_ref[...] = projected - projected[:, LAST:BINS]
+
+
+def pack_kernel(scores_ref, code_ref, code_other, send, own):
+    core = lax.axis_index("co")
+    first = core == 0
+    mine, other = code_ref[...], code_other[...]
+    pair = lax.broadcasted_iota(jnp.int32, (HALF, ROWS), 0)
+    row = lax.broadcasted_iota(jnp.int32, (HALF, ROWS), 1)
+    spread = jnp.where(pair // COLS + 16 * core == row, 1.0, 0.0).astype(BF16)
+    codes = (jnp.where(first, mine, other), jnp.where(first, other, mine))
+    by_row = jnp.concatenate([product(spread, code.astype(BF16), 1, 1) for code in codes], axis=0)
+    pair = lax.broadcasted_iota(jnp.int32, (PAIRS, COLS), 0)
+    col = lax.broadcasted_iota(jnp.int32, (PAIRS, COLS), 1)
+    code = jnp.sum(jnp.where(pair % COLS == col, by_row, 0.0), axis=1, keepdims=True)
+    scored = jnp.where(code >= 64.0, 1.0, 0.0)
     lane = lax.broadcasted_iota(jnp.int32, (PAIRS, C), 1)
-    projected = projected - projected[:, LAST:BINS]
-    projected = jnp.where(lane < LAST, projected, jnp.where(lane == LAST, code - 64.0 * scored, scored))
+    projected = jnp.where(lane < LAST, scores_ref[...], jnp.where(lane == LAST, code - 64.0 * scored, scored))
     own[...] = projected
     send[...] = jnp.where(lane[:HALF] < BINS, projected[:HALF], pltpu.roll(projected[HALF:], BINS, 1))
 
@@ -306,25 +311,28 @@
     swap = [(0, 1), (1, 0)]
     x = pair_rep.reshape(PAIRS, C)
     gain, bias, w_pde, labels, mask = ln_gain.reshape(1, C), ln_bias.reshape(1, C), w_pde.T, labels.T, pair_mask.T
-    x_other, labels_other, mask_other = (lax.ppermute(a, "co", swap) for a in (x, labels, mask))
+    x_other = lax.ppermute(x, "co", swap)
     full, half = (PAIRS, C), (PAIRS, H)
     in_hbm = functools.partial(pltpu.with_memory_space_constraint, memory_space=pltpu.HBM)
-    x, gain, bias, labels, mask, *weights = call(
+    x, gain, bias, code, *weights = call(
         load_kernel,
-        [(HALF, C), (1, C), (1, C), ((COLS, ROWS), jnp.int32), ((COLS, ROWS), jnp.int32), (BINS, C)]
+        [(HALF, C), (1, C), (1, C), (COLS, ROWS), (BINS, C)]
         + [((2 * H, C), BF16)] * 2
         + [((H, C), BF16)] * 2,
         [HBM] * 8,
-        scratch=[pltpu.VMEM((2 * H, C), F32), pltpu.VMEM((H, C), F32), pltpu.SemaphoreType.DMA((8,))],
+        scratch=[pltpu.VMEM((2 * H, C), F32), pltpu.VMEM((H, C), F32)]
+        + [pltpu.VMEM((COLS, ROWS), jnp.int32)] * 2
+        + [pltpu.SemaphoreType.DMA((8,))],
         name="load",
     )(*(in_hbm(a) for a in (x, gain, bias, labels, mask, w_pde, w_in, w_out)))
-    send, *kept = call(
+    code_other = lax.ppermute(code, "co", swap)
+    scores, *kept = call(
         forward_kernel,
-        [(HALF, C), full, (full, BF16), (full, BF16), full, full, (full, BF16), (full, BF16)]
-        + [half, half, (half, BF16), (half, BF16)],
-        [VMEM] * 13,
+        [full, (full, BF16), (full, BF16), full, full, (full, BF16), (full, BF16)] + [half, half, (half, BF16), (half, BF16)],
+        [VMEM] * 9,
         name="forward",
-    )(x_other, labels_other, mask_other, x, gain, bias, labels, mask, *weights)
+    )(x_other, x, gain, bias, *weights)
+    send, own = call(pack_kernel, [(HALF, C), full], [VMEM] * 3, name="pack")(scores, code, code_other)
     received = lax.ppermute(send, AXES, mirror_pairs())
     send, keep, d_x = call(
         backward_kernel,
@@ -332,7 +340,7 @@
         [VMEM] * 18,
         scratch=[pltpu.VMEM(full, F32)] * 2,
         name="backward",
-    )(received, gain, *weights, *kept)
+    )(received, gain, *weights, own, *kept)
     from_core = lax.ppermute(send, "co", swap)
     (send,) = call(core_sum_kernel, [(16, BIG + SMALL, C)], [VMEM] * 2, name="core_sum")(keep, from_core)
     received = lax.all_to_all(send, PLANE, 0, 0, tiled=True)

time: 63.3 us -> 63.2 us (level)
    ppermute x3 -> x2, starting transfers between devices: 3.92 us -> 3.43 us  [the longest x1 3.33 us: on_device(): x_other = lax.ppermute(x, 'co', swap)]
    pallas_call x2 -> x3, Pallas kernels: 2.53 us -> 2.75 us  [the longest x1 1.23 us: on_device(): call(load_kernel, [(HALF, C), (1, C), (1, C), (COLS, ROWS), (BINS, C)] +...]
  transfers between devices with their start and end apart: 6 -> 5, of which waited for: 3 -> 3; matrix products, arithmetic and copies ran while one was open for 0% -> 0% of each run, Pallas kernels for 3% -> 5%
where the time goes in v6:
time: 63.2 us; the launch traced here: 63 us
  blocking collectives  40.5 us (64%)
  starting transfers between devices  10.1 us (16%)
  Pallas kernels  6.31 us (10%)
  waiting for transfers between devices  5.42 us (9%)
  between operations  0.7 us (1%)
    all_to_all x1, blocking collectives, on_device(): received = lax.all_to_all(send, PLANE, 0, 0, tiled=True)  24.9 us
    all_to_all x1, blocking collectives, on_device(): received = lax.all_to_all(send, 'z', 0, 0, tiled=True)  15.6 us
    ppermute x1, waiting for transfers between devices, on_device(): received = lax.ppermute(send, AXES, mirror_pairs())  3.63 us
    ppermute x1, starting transfers between devices, on_device(): received = lax.ppermute(send, AXES, mirror_pairs())  3.45 us
    ppermute x1, starting transfers between devices, on_device(): x_other = lax.ppermute(x, 'co', swap)  3.33 us
    ppermute x1, starting transfers between devices, on_device(): other = lax.ppermute(d_pde, 'co', swap)  3.1 us
    pallas_call x1, Pallas kernels, on_device(): call(backward_kernel, [(SLAB + HALF, C), (SLAB, C), (HALF, C)], [VMEM] *...  1.87 us
    ppermute x1, waiting for transfers between devices, on_device(): from_core = lax.ppermute(send, 'co', swap)  1.74 us
  transfers between devices with their start and end apart: 5, of which 3 were waited for; matrix products, arithmetic and copies ran while one was open for 0% of the time, Pallas kernels for 5%

profile of v6, /device:TPU:1, one launch (start us, length us, event | category | flops | bytes accessed | tf_op | source)
XLA Modules:
  0.0 63.0 jit_solution(2292187381169424782)
XLA Ops:
  0.6 3.3 %collective-permute-start = (f32[256,128]{1,0:T(8,128)}, f32[256,128]{1,0:T(8,128)S(1)}, u32[]{:S(2)}, u32[]{:S(2)}) collective-permute-start(f32[256,128]{1,0:T(8,128)} %bitcast.11), channel_id=1, source_target_pairs={{0,1},{1,0},{2,3},{3,2},{4,5},{5,4},{6,7},{7,6},{8,9},{9,8},{10,11... | collective-permute-start | bytes 393224 | tf_op jit(solution)/shard_map/ppermute | solution.py:314
  4.0 1.2 %load.1 = (f32[128,128]{1,0:T(8,128)S(1)}, f32[1,128]{1,0:T(1,128)S(1)}, f32[1,128]{1,0:T(1,128)S(1)}, f32[8,32]{1,0:T(8,128)S(1)}, f32[64,128]{1,0:T(8,128)S(1)...) custom-call(f32[256,128]{1,0:T(8,128)} %bitcast.12, ...), custom_call_target="tpu_custom_call" | custom-call | tf_op jit(solution)/shard_map/load/pallas_call | solution.py:317
  5.2 0.1 collective-permute-start.1
  5.3 0.0 collective-permute-done.x_other
  5.3 1.2 %forward.1 = (f32[256,128]{1,0:T(8,128)S(1)}, bf16[256,128]{1,0:T(8,128)(2,1)S(1)}, bf16[256,128]{1,0:T(8,128)(2,1)S(1)}, f32[256,128]{1,0:T(8,128)S(1)}, f32[25...) custom-call(f32[256,128]{1,0:T(8,128)S(1)} %collective-permute-done., ...), custom_call_target="tpu_custom_call" | custom-call | tf_op jit(solution)/shard_map/forward/pallas_call | solution.py:329
  6.5 0.0 collective-permute-done.1.code_other
  6.5 0.3 pack.1
  6.8 3.5 %collective-permute-start.2 = (f32[128,128]{1,0:T(8,128)S(1)}, f32[128,128]{1,0:T(8,128)S(1)}, u32[]{:S(2)}, u32[]{:S(2)}) collective-permute-start(f32[128,128]{1,0:T(8,128)S(1)} %get-tuple-element.48), channel_id=1, source_target_pairs={{0,0},{1,2},{2,1},{3,3},{4,32},{5,34},{6,33},{7,35},{8,64},{9,66},... | collective-permute-start | bytes 196616 | tf_op jit(solution)/shard_map/ppermute | solution.py:336
  10.3 3.6 %collective-permute-done.2.received = f32[128,128]{1,0:T(8,128)S(1)} collective-permute-done((f32[128,128]{1,0:T(8,128)S(1)}, f32[128,128]{1,0:T(8,128)S(1)}, u32[]{:S(2)}, u32[]{:S(2)}) %collective-permute-start.2) | collective-permute-done | bytes 65568 | tf_op jit(solution)/shard_map/ppermute | solution.py:336
  13.9 1.9 %backward.1 = (f32[808,128]{1,0:T(8,128)S(1)}, f32[680,128]{1,0:T(8,128)S(1)}, f32[128,128]{1,0:T(8,128)S(1)}) custom-call(f32[128,128]{1,0:T(8,128)S(1)} %collective-permute-done.2.received, f32[1,128]{1,0:T(1,128)S(1)} %get-tuple-element.39.gain, f32[64,128]{1,0:T(8,128)S(1)} %get-tuple-element.41.w_pde, bf16[1024,128]{1,0:T(8,128)(2,1)S(1)} %get-tuple-element.42.in_high, ...), custom_call_target="tpu_custom_call" | custom-call | tf_op jit(solution)/shard_map/backward/pallas_call | solution.py:337
  15.8 0.1 collective-permute-start.3
  15.9 1.7 %collective-permute-done.3.received.d_x_other = f32[808,128]{1,0:T(8,128)S(1)} collective-permute-done((f32[808,128]{1,0:T(8,128)S(1)}, f32[808,128]{1,0:T(8,128)S(1)}, u32[]{:S(2)}, u32[]{:S(2)}) %collective-permute-start.3) | collective-permute-done | bytes 413728 | tf_op jit(solution)/shard_map/ppermute | solution.py:344
  17.7 24.9 %all_to_all.10.received = f32[16,80,128]{2,1,0:T(8,128)S(1)} all-to-all(f32[16,80,128]{2,1,0:T(8,128)S(1)} %core_sum.1), channel_id=1, replica_groups=mesh['yl'=2,'x'=4,'z'=8,'yh'=2,'co'=2] {'yl','x','yh'}, dimensions={0} | all-to-all | bytes 1310720 | tf_op jit(solution)/shard_map/all_to_all | solution.py:346
  42.6 0.1 plane_sum.1
  42.7 15.6 %all_to_all.11.received = f32[8,40,128]{2,1,0:T(8,128)S(1)} all-to-all(f32[8,40,128]{2,1,0:T(8,128)S(1)} %plane_sum.1), channel_id=1, replica_groups=mesh['yl'=2,'x'=4,'z'=8,'yh'=2,'co'=2] {'z'}, dimensions={0} | all-to-all | bytes 327680 | tf_op jit(solution)/shard_map/all_to_all | solution.py:348
  58.3 0.1 pde_sum.1.mine
  58.4 3.1 %collective-permute-start.4 = (f32[32,128]{1,0:T(8,128)S(1)}, f32[32,128]{1,0:T(8,128)S(1)}, u32[]{:S(2)}, u32[]{:S(2)}) collective-permute-start(f32[32,128]{1,0:T(8,128)S(1)} %pde_sum.1.mine), channel_id=1, source_target_pairs={{0,1},{1,0},{2,3},{3,2},{4,5},{5,4},{6,7},{7,6},{8,9},{9,8},{10,11... | collective-permute-start | bytes 49160 | tf_op jit(solution)/shard_map/ppermute | solution.py:350
  61.5 0.8 %column_sum.1 = (f32[1,1]{1,0:T(1,128)}, f32[1,128]{1,0:T(1,128)}, f32[1,128]{1,0:T(1,128)}, f32[4,128]{1,0:T(4,128)}, f32[2,128]{1,0:T(2,128)}, /*index=5*/f32[256,128]{1,0:T(8,128)}) custom-call(f32[8,40,128]{2,1,0:T(8,128)S(1)} %all_to_all.11.received, f32[64,128]{1,0:T(8,128)S(1)} %get-tuple-element.41.w_pde, f32[128,128]{1,0:T(8,128)S(1)} %get-tuple-element.62.d_x, ...), custom_call_target="tpu_custom_call" | custom-call | tf_op jit(solution)/shard_map/column_sum/pallas_call | solution.py:351
  62.3 0.1 collective-permute-done.4.other
  62.3 0.6 join.1
  (1 shorter events, 0.0 us)
Async XLA Ops:
  0.6 4.7 %collective-permute-start = (f32[256,128]{1,0:T(8,128)}, f32[256,128]{1,0:T(8,128)S(1)}, u32[]{:S(2)}, u32[]{:S(2)}) collective-permute-start(f32[256,128]{1,0:T(8,128)} %bitcast.11), channel_id=1, source_target_pairs={{0,1},{1,0},{2,3},{3,2},{4,5},{5,4},{6,7},{7,6},{8,9},{9,8},{10,11... | collective-permute-start | bytes 393224 | tf_op jit(solution)/shard_map/ppermute | solution.py:314
  5.2 1.3 %collective-permute-start.1 = (f32[8,32]{1,0:T(8,128)S(1)}, f32[8,32]{1,0:T(8,128)S(1)}, u32[]{:S(2)}, u32[]{:S(2)}) collective-permute-start(f32[8,32]{1,0:T(8,128)S(1)} %get-tuple-element.47.code_ref), channel_id=1, source_target_pairs={{0,1},{1,0},{2,3},{3,2},{4,5},{5,4},{6,7},{7,6},{8,9},{9,8},{10,11... | collective-permute-start | bytes 3080 | tf_op jit(solution)/shard_map/ppermute | solution.py:328
  6.8 7.1 %collective-permute-start.2 = (f32[128,128]{1,0:T(8,128)S(1)}, f32[128,128]{1,0:T(8,128)S(1)}, u32[]{:S(2)}, u32[]{:S(2)}) collective-permute-start(f32[128,128]{1,0:T(8,128)S(1)} %get-tuple-element.48), channel_id=1, source_target_pairs={{0,0},{1,2},{2,1},{3,3},{4,32},{5,34},{6,33},{7,35},{8,64},{9,66},... | collective-permute-start | bytes 196616 | tf_op jit(solution)/shard_map/ppermute | solution.py:336
  15.8 1.8 %collective-permute-start.3 = (f32[808,128]{1,0:T(8,128)S(1)}, f32[808,128]{1,0:T(8,128)S(1)}, u32[]{:S(2)}, u32[]{:S(2)}) collective-permute-start(f32[808,128]{1,0:T(8,128)S(1)} %get-tuple-element.61), channel_id=1, source_target_pairs={{0,1},{1,0},{2,3},{3,2},{4,5},{5,4},{6,7},{7,6},{8,9},{9,8},{10,11... | collective-permute-start | bytes 1241096 | tf_op jit(solution)/shard_map/ppermute | solution.py:344
  58.4 3.9 %collective-permute-start.4 = (f32[32,128]{1,0:T(8,128)S(1)}, f32[32,128]{1,0:T(8,128)S(1)}, u32[]{:S(2)}, u32[]{:S(2)}) collective-permute-start(f32[32,128]{1,0:T(8,128)S(1)} %pde_sum.1.mine), channel_id=1, source_target_pairs={{0,1},{1,0},{2,3},{3,2},{4,5},{5,4},{6,7},{7,6},{8,9},{9,8},{10,11... | collective-permute-start | bytes 49160 | tf_op jit(solution)/shard_map/ppermute | solution.py:350

commit v7 on v5

--- a/solution.py
+++ b/solution.py
@@ -19,7 +19,6 @@
 HALF = PAIRS // 2
 F32, BF16 = jnp.float32, jnp.bfloat16
 LAST = BINS - 1
-MASK = BINS
 BIG = 40
 SMALL = 40
 SLAB = 16 * BIG + SMALL
@@ -69,9 +68,27 @@
         copy.wait()
 
 
+def spread_pairs(mine, other):
+    core = lax.axis_index("co")
+    first = core == 0
+    pair = lax.broadcasted_iota(jnp.int32, (HALF, ROWS), 0)
+    row = lax.broadcasted_iota(jnp.int32, (HALF, ROWS), 1)
+    spread = jnp.where(pair // COLS + 16 * core == row, 1.0, 0.0).astype(BF16)
+    mine, other = mine.astype(F32), other.astype(F32)
+    parts = (jnp.where(first, mine, other), jnp.where(first, other, mine))
+    by_row = jnp.concatenate([product(spread, part.astype(BF16), 1, 1) for part in parts], axis=0)
+    pair = lax.broadcasted_iota(jnp.int32, (PAIRS, COLS), 0)
+    col = lax.broadcasted_iota(jnp.int32, (PAIRS, COLS), 1)
+    return jnp.sum(jnp.where(pair % COLS == col, by_row, 0.0), axis=1, keepdims=True)
+
+
+def scored_kernel(mask, mask_other, scored):
+    scored[...] = jnp.broadcast_to(spread_pairs(mask[...], mask_other[...]), (PAIRS, C))
+
+
 def forward_kernel(
-    x_other, labels_other, mask_other, x_ref, gain, bias, labels, mask, w_pde, in_high, in_low, out_high, out_low,
-    send, own, updated_high, updated_low, unit_ref, scale_ref, normed_high, normed_low,
+    x_other, labels_other, x_ref, gain, bias, labels, mask, w_pde, in_high, in_low, out_high, out_low,
+    send, mask_out, own, updated_high, updated_low, unit_ref, scale_ref, normed_high, normed_low,
     silu_ref, slope_ref, hidden_high, hidden_low,
 ):
     core = lax.axis_index("co")
@@ -84,17 +101,8 @@
     scale_ref[...] = jnp.broadcast_to(scale, (PAIRS, C))
     normed = split(unit * gain[...] + bias[...])
     normed_high[...], normed_low[...] = normed
-    mine = (labels[...] + 64 * mask[...]).astype(F32)
-    other = (labels_other[...] + 64 * mask_other[...]).astype(F32)
-    pair = lax.broadcasted_iota(jnp.int32, (HALF, ROWS), 0)
-    row = lax.broadcasted_iota(jnp.int32, (HALF, ROWS), 1)
-    spread = jnp.where(pair // COLS + 16 * core == row, 1.0, 0.0).astype(BF16)
-    codes = (jnp.where(first, mine, other), jnp.where(first, other, mine))
-    by_row = jnp.concatenate([product(spread, code.astype(BF16), 1, 1) for code in codes], axis=0)
-    pair = lax.broadcasted_iota(jnp.int32, (PAIRS, COLS), 0)
-    col = lax.broadcasted_iota(jnp.int32, (PAIRS, COLS), 1)
-    code = jnp.sum(jnp.where(pair % COLS == col, by_row, 0.0), axis=1, keepdims=True)
-    scored = jnp.where(code >= 64.0, 1.0, 0.0)
+    mask_out[...] = mask[...]
+    label = spread_pairs(labels[...], labels_other[...])
     projected_in = deep(normed, (in_high[...], in_low[...]), 1)
     gate, up = projected_in[:, :H], projected_in[:, H:]
     sigmoid = 1.0 / (1.0 + jnp.exp(-gate))
@@ -113,13 +121,13 @@
     projected = projected + pltpu.roll(projected, BINS, 1)
     lane = lax.broadcasted_iota(jnp.int32, (PAIRS, C), 1)
     projected = projected - projected[:, LAST:BINS]
-    projected = jnp.where(lane < LAST, projected, jnp.where(lane == LAST, code - 64.0 * scored, scored))
+    projected = jnp.where(lane < LAST, projected, label)
     own[...] = projected
     send[...] = jnp.where(lane[:HALF] < BINS, projected[:HALF], pltpu.roll(projected[HALF:], BINS, 1))
 
 
 def backward_kernel(
-    received, gain, w_pde, in_high, in_low, out_high, out_low, own, updated_high, updated_low, unit_ref, scale_ref,
+    received, scored_ref, gain, w_pde, in_high, in_low, out_high, out_low, own, updated_high, updated_low, unit_ref, scale_ref,
     normed_high, normed_low, silu_ref, slope_ref, hidden_high, hidden_low,
     send, keep, d_x_ref, flat_ref, mirrored_ref,
 ):
@@ -134,7 +142,7 @@
     mine, mirrored = own[...], mirrored_ref[...]
     lane = lax.broadcasted_iota(jnp.int32, (PAIRS, C), 1)
     lane_float = lane.astype(jnp.float32)
-    scored = mine[:, MASK : MASK + 1]
+    scored = scored_ref[:, 0:1]
     onehot = lane_float == mine[:, LAST:BINS]
     onehot_mirrored = lane_float == mirrored[:, LAST:BINS]
     scores = jnp.where(lane < LAST, mine + mirrored, jnp.where(lane == LAST, 0.0, -jnp.inf))
@@ -306,7 +314,7 @@
     swap = [(0, 1), (1, 0)]
     x = pair_rep.reshape(PAIRS, C)
     gain, bias, w_pde, labels, mask = ln_gain.reshape(1, C), ln_bias.reshape(1, C), w_pde.T, labels.T, pair_mask.T
-    x_other, labels_other, mask_other = (lax.ppermute(a, "co", swap) for a in (x, labels, mask))
+    x_other, labels_other = (lax.ppermute(a, "co", swap) for a in (x, labels))
     full, half = (PAIRS, C), (PAIRS, H)
     in_hbm = functools.partial(pltpu.with_memory_space_constraint, memory_space=pltpu.HBM)
     x, gain, bias, labels, mask, *weights = call(
@@ -318,21 +326,23 @@
         scratch=[pltpu.VMEM((2 * H, C), F32), pltpu.VMEM((H, C), F32), pltpu.SemaphoreType.DMA((8,))],
         name="load",
     )(*(in_hbm(a) for a in (x, gain, bias, labels, mask, w_pde, w_in, w_out)))
-    send, *kept = call(
+    send, mask, *kept = call(
         forward_kernel,
-        [(HALF, C), full, (full, BF16), (full, BF16), full, full, (full, BF16), (full, BF16)]
+        [(HALF, C), ((COLS, ROWS), jnp.int32), full, (full, BF16), (full, BF16), full, full, (full, BF16), (full, BF16)]
         + [half, half, (half, BF16), (half, BF16)],
-        [VMEM] * 13,
+        [VMEM] * 12,
         name="forward",
-    )(x_other, labels_other, mask_other, x, gain, bias, labels, mask, *weights)
+    )(x_other, labels_other, x, gain, bias, labels, mask, *weights)
     received = lax.ppermute(send, AXES, mirror_pairs())
+    mask_other = lax.ppermute(mask, "co", swap)
+    (scored,) = call(scored_kernel, [full], [VMEM] * 2, name="scored")(mask, mask_other)
     send, keep, d_x = call(
         backward_kernel,
         [(SLAB + HALF, C), (SLAB, C), (HALF, C)],
-        [VMEM] * 18,
+        [VMEM] * 19,
         scratch=[pltpu.VMEM(full, F32)] * 2,
         name="backward",
-    )(received, gain, *weights, *kept)
+    )(received, scored, gain, *weights, *kept)
     from_core = lax.ppermute(send, "co", swap)
     (send,) = call(core_sum_kernel, [(16, BIG + SMALL, C)], [VMEM] * 2, name="core_sum")(keep, from_core)
     received = lax.all_to_all(send, PLANE, 0, 0, tiled=True)

time: 63.3 us -> 62.8 us (level)
  waiting for transfers between devices: 5.89 us -> 5.2 us
    ppermute x1, waiting for transfers between devices: 4.09 us -> 2.22 us  [on_device(): received = lax.ppermute(send, AXES, mirror_pairs())]
    ppermute x3, waiting for transfers between devices: 0.01 us -> 1.19 us  [the longest x1 1.15 us: on_device(): mask_other = lax.ppermute(mask, 'co', swap)]
    pallas_call x1 -> x2, Pallas kernels: 1.3 us -> 1.51 us  [the longest x1 1.28 us: on_device(): call(forward_kernel, [(HALF, C), ((COLS, ROWS), jnp.int32), full, (full,...]
  transfers between devices with their start and end apart: 6 -> 6, of which waited for: 3 -> 4; matrix products, arithmetic and copies ran while one was open for 0% -> 0% of each run, Pallas kernels for 3% -> 4%
where the time goes in v7:
time: 62.8 us; the launch traced here: 62.6 us
  blocking collectives  40.4 us (64%)
  starting transfers between devices  10.1 us (16%)
  Pallas kernels  6.23 us (10%)
  waiting for transfers between devices  5.2 us (8%)
  between operations  0.7 us (1%)
    all_to_all x1, blocking collectives, on_device(): received = lax.all_to_all(send, PLANE, 0, 0, tiled=True)  24.8 us
    all_to_all x1, blocking collectives, on_device(): received = lax.all_to_all(send, 'z', 0, 0, tiled=True)  15.6 us
    ppermute x2, starting transfers between devices, on_device(): x_other, labels_other = (lax.ppermute(a, 'co', swap) for a in (x, labels))  3.43 us
    ppermute x1, starting transfers between devices, on_device(): received = lax.ppermute(send, AXES, mirror_pairs())  3.38 us
    ppermute x1, starting transfers between devices, on_device(): other = lax.ppermute(d_pde, 'co', swap)  3.1 us
    ppermute x1, waiting for transfers between devices, on_device(): received = lax.ppermute(send, AXES, mirror_pairs())  2.22 us
    pallas_call x1, Pallas kernels, on_device(): call(backward_kernel, [(SLAB + HALF, C), (SLAB, C), (HALF, C)], [VMEM] *...  1.8 us
    ppermute x1, waiting for transfers between devices, on_device(): from_core = lax.ppermute(send, 'co', swap)  1.74 us
  transfers between devices with their start and end apart: 6, of which 4 were waited for; matrix products, arithmetic and copies ran while one was open for 0% of the time, Pallas kernels for 4%

profile of v7, /device:TPU:1, one launch (start us, length us, event | category | flops | bytes accessed | tf_op | source)
XLA Modules:
  0.0 62.6 jit_solution(2572679035364893441)
XLA Ops:
  0.6 3.3 %collective-permute-start = (f32[256,128]{1,0:T(8,128)}, f32[256,128]{1,0:T(8,128)S(1)}, u32[]{:S(2)}, u32[]{:S(2)}) collective-permute-start(f32[256,128]{1,0:T(8,128)} %bitcast.11), channel_id=1, source_target_pairs={{0,1},{1,0},{2,3},{3,2},{4,5},{5,4},{6,7},{7,6},{8,9},{9,8},{10,11... | collective-permute-start | bytes 393224 | tf_op jit(solution)/shard_map/ppermute | solution.py:317
  4.0 0.1 collective-permute-start.1
  4.1 1.2 %load.1 = (f32[128,128]{1,0:T(8,128)S(1)}, f32[1,128]{1,0:T(1,128)S(1)}, f32[1,128]{1,0:T(1,128)S(1)}, s32[8,32]{1,0:T(8,128)S(1)}, s32[8,32]{1,0:T(8,128)S(1)},...) custom-call(f32[256,128]{1,0:T(8,128)} %bitcast.12, ...), custom_call_target="tpu_custom_call" | custom-call | tf_op jit(solution)/shard_map/load/pallas_call | solution.py:320
  5.3 0.0 collective-permute-done.1.labels_other
  5.3 0.0 collective-permute-done.x_other
  5.3 1.3 %forward.1 = (f32[128,128]{1,0:T(8,128)S(1)}, s32[8,32]{1,0:T(8,128)S(1)}, f32[256,128]{1,0:T(8,128)S(1)}, bf16[256,128]{1,0:T(8,128)(2,1)S(1)}, bf16[256,128]{1...) custom-call(f32[256,128]{1,0:T(8,128)S(1)} %collective-permute-done., ...), custom_call_target="tpu_custom_call" | custom-call | tf_op jit(solution)/shard_map/forward/pallas_call | solution.py:329
  6.6 3.4 %collective-permute-start.2 = (f32[128,128]{1,0:T(8,128)S(1)}, f32[128,128]{1,0:T(8,128)S(1)}, u32[]{:S(2)}, u32[]{:S(2)}) collective-permute-start(f32[128,128]{1,0:T(8,128)S(1)} %get-tuple-element.49), channel_id=1, source_target_pairs={{0,0},{1,2},{2,1},{3,3},{4,32},{5,34},{6,33},{7,35},{8,64},{9,66},... | collective-permute-start | bytes 196616 | tf_op jit(solution)/shard_map/ppermute | solution.py:336
  10.0 0.1 collective-permute-start.3
  10.1 1.2 %collective-permute-done.3.mask_other = s32[8,32]{1,0:T(8,128)S(1)} collective-permute-done((s32[8,32]{1,0:T(8,128)S(1)}, s32[8,32]{1,0:T(8,128)S(1)}, u32[]{:S(2)}, u32[]{:S(2)}) %collective-permute-start.3) | collective-permute-done | bytes 1056 | tf_op jit(solution)/shard_map/ppermute | solution.py:337
  11.3 0.2 scored.1.scored_ref
  11.5 2.2 %collective-permute-done.2.received = f32[128,128]{1,0:T(8,128)S(1)} collective-permute-done((f32[128,128]{1,0:T(8,128)S(1)}, f32[128,128]{1,0:T(8,128)S(1)}, u32[]{:S(2)}, u32[]{:S(2)}) %collective-permute-start.2) | collective-permute-done | bytes 65568 | tf_op jit(solution)/shard_map/ppermute | solution.py:336
  13.7 1.8 %backward.1 = (f32[808,128]{1,0:T(8,128)S(1)}, f32[680,128]{1,0:T(8,128)S(1)}, f32[128,128]{1,0:T(8,128)S(1)}) custom-call(f32[128,128]{1,0:T(8,128)S(1)} %collective-permute-done.2.received, f32[256,128]{1,0:T(8,128)S(1)} %scored.1.scored_ref, f32[1,128]{1,0:T(1,128)S(1)} %get-tuple-element.40.gain, f32[64,128]{1,0:T(8,128)S(1)} %get-tuple-element.44.w_pde, ...), custom_call_target="tpu_custom_call" | custom-call | tf_op jit(solution)/shard_map/backward/pallas_call | solution.py:339
  15.5 0.1 collective-permute-start.4
  15.6 1.7 %collective-permute-done.4.received.d_x_other = f32[808,128]{1,0:T(8,128)S(1)} collective-permute-done((f32[808,128]{1,0:T(8,128)S(1)}, f32[808,128]{1,0:T(8,128)S(1)}, u32[]{:S(2)}, u32[]{:S(2)}) %collective-permute-start.4) | collective-permute-done | bytes 413728 | tf_op jit(solution)/shard_map/ppermute | solution.py:346
  17.4 24.8 %all_to_all.10.received = f32[16,80,128]{2,1,0:T(8,128)S(1)} all-to-all(f32[16,80,128]{2,1,0:T(8,128)S(1)} %core_sum.1), channel_id=1, replica_groups=mesh['yl'=2,'x'=4,'z'=8,'yh'=2,'co'=2] {'yl','x','yh'}, dimensions={0} | all-to-all | bytes 1310720 | tf_op jit(solution)/shard_map/all_to_all | solution.py:348
  42.2 0.1 plane_sum.1
  42.4 15.6 %all_to_all.11.received = f32[8,40,128]{2,1,0:T(8,128)S(1)} all-to-all(f32[8,40,128]{2,1,0:T(8,128)S(1)} %plane_sum.1), channel_id=1, replica_groups=mesh['yl'=2,'x'=4,'z'=8,'yh'=2,'co'=2] {'z'}, dimensions={0} | all-to-all | bytes 327680 | tf_op jit(solution)/shard_map/all_to_all | solution.py:350
  57.9 0.1 pde_sum.1.mine
  58.0 3.1 %collective-permute-start.5 = (f32[32,128]{1,0:T(8,128)S(1)}, f32[32,128]{1,0:T(8,128)S(1)}, u32[]{:S(2)}, u32[]{:S(2)}) collective-permute-start(f32[32,128]{1,0:T(8,128)S(1)} %pde_sum.1.mine), channel_id=1, source_target_pairs={{0,1},{1,0},{2,3},{3,2},{4,5},{5,4},{6,7},{7,6},{8,9},{9,8},{10,11... | collective-permute-start | bytes 49160 | tf_op jit(solution)/shard_map/ppermute | solution.py:352
  61.1 0.8 %column_sum.1 = (f32[1,1]{1,0:T(1,128)}, f32[1,128]{1,0:T(1,128)}, f32[1,128]{1,0:T(1,128)}, f32[4,128]{1,0:T(4,128)}, f32[2,128]{1,0:T(2,128)}, /*index=5*/f32[256,128]{1,0:T(8,128)}) custom-call(f32[8,40,128]{2,1,0:T(8,128)S(1)} %all_to_all.11.received, f32[64,128]{1,0:T(8,128)S(1)} %get-tuple-element.44.w_pde, f32[128,128]{1,0:T(8,128)S(1)} %get-tuple-element.64.d_x, ...), custom_call_target="tpu_custom_call" | custom-call | tf_op jit(solution)/shard_map/column_sum/pallas_call | solution.py:353
  61.9 0.1 collective-permute-done.5.other
  62.0 0.6 join.1
  (1 shorter events, 0.0 us)
Async XLA Ops:
  0.6 4.7 %collective-permute-start = (f32[256,128]{1,0:T(8,128)}, f32[256,128]{1,0:T(8,128)S(1)}, u32[]{:S(2)}, u32[]{:S(2)}) collective-permute-start(f32[256,128]{1,0:T(8,128)} %bitcast.11), channel_id=1, source_target_pairs={{0,1},{1,0},{2,3},{3,2},{4,5},{5,4},{6,7},{7,6},{8,9},{9,8},{10,11... | collective-permute-start | bytes 393224 | tf_op jit(solution)/shard_map/ppermute | solution.py:317
  4.0 1.4 %collective-permute-start.1 = (s32[8,32]{1,0:T(8,128)}, s32[8,32]{1,0:T(8,128)S(1)}, u32[]{:S(2)}, u32[]{:S(2)}) collective-permute-start(s32[8,32]{1,0:T(8,128)} %bitcast.16), channel_id=1, source_target_pairs={{0,1},{1,0},{2,3},{3,2},{4,5},{5,4},{6,7},{7,6},{8,9},{9,8},{10,11... | collective-permute-start | bytes 3080 | tf_op jit(solution)/shard_map/ppermute | solution.py:317
  6.6 7.1 %collective-permute-start.2 = (f32[128,128]{1,0:T(8,128)S(1)}, f32[128,128]{1,0:T(8,128)S(1)}, u32[]{:S(2)}, u32[]{:S(2)}) collective-permute-start(f32[128,128]{1,0:T(8,128)S(1)} %get-tuple-element.49), channel_id=1, source_target_pairs={{0,0},{1,2},{2,1},{3,3},{4,32},{5,34},{6,33},{7,35},{8,64},{9,66},... | collective-permute-start | bytes 196616 | tf_op jit(solution)/shard_map/ppermute | solution.py:336
  10.0 1.3 %collective-permute-start.3 = (s32[8,32]{1,0:T(8,128)S(1)}, s32[8,32]{1,0:T(8,128)S(1)}, u32[]{:S(2)}, u32[]{:S(2)}) collective-permute-start(s32[8,32]{1,0:T(8,128)S(1)} %get-tuple-element.50.mask), channel_id=1, source_target_pairs={{0,1},{1,0},{2,3},{3,2},{4,5},{5,4},{6,7},{7,6},{8,9},{9,8},{10,11... | collective-permute-start | bytes 3080 | tf_op jit(solution)/shard_map/ppermute | solution.py:337
  15.5 1.8 %collective-permute-start.4 = (f32[808,128]{1,0:T(8,128)S(1)}, f32[808,128]{1,0:T(8,128)S(1)}, u32[]{:S(2)}, u32[]{:S(2)}) collective-permute-start(f32[808,128]{1,0:T(8,128)S(1)} %get-tuple-element.63), channel_id=1, source_target_pairs={{0,1},{1,0},{2,3},{3,2},{4,5},{5,4},{6,7},{7,6},{8,9},{9,8},{10,11... | collective-permute-start | bytes 1241096 | tf_op jit(solution)/shard_map/ppermute | solution.py:346
  58.0 3.9 %collective-permute-start.5 = (f32[32,128]{1,0:T(8,128)S(1)}, f32[32,128]{1,0:T(8,128)S(1)}, u32[]{:S(2)}, u32[]{:S(2)}) collective-permute-start(f32[32,128]{1,0:T(8,128)S(1)} %pde_sum.1.mine), channel_id=1, source_target_pairs={{0,1},{1,0},{2,3},{3,2},{4,5},{5,4},{6,7},{7,6},{8,9},{9,8},{10,11... | collective-permute-start | bytes 49160 | tf_op jit(solution)/shard_map/ppermute | solution.py:352
